TPU v7x, 256 devices: a whole 4x4x8 slice. The times are simulated.
256 devices in a mesh: slide: 16 (over y, x), row: 4 (over z_hi, core), col: 4 (over z_lo).
Axes of the slice: x: 4, y: 4, z: 8 (z_hi: 2, z_lo: 4; z = z_hi * 4 + z_lo), core: 2. Of those that a mesh axis runs over, the one named last changes fastest.
Arguments:
- features: bfloat16 [16, 256, 512, 256], P('slide', 'row', 'col'), may hold values from -6 to 6
- out_grad: bfloat16 [16, 256, 512, 256], P('slide', 'row', 'col'), may hold values from -6 to 6
- depth_weight: bfloat16 [9, 256], replicated, may hold values from -2 to 2
- point_weight: bfloat16 [256, 256], P(('slide', 'row', 'col')), may hold values from -0.375 to 0.375
Outputs:
- feature_grad: bfloat16 [16, 256, 512, 256], P('slide', 'row', 'col')
- point_grad: float32 [256, 256], P(('slide', 'row', 'col'))
- depth_grad: float32 [9, 256], replicated
All inputs are finite; a program needn't handle non-finite values.
Results may differ from a plain program's by a relative error of at most 0.007.
Values may be sent and summed in bfloat16 or wider, within the bound.
No kernel may reach another device: no remote copies, remote signals or barrier semaphores. Data moves between devices by JAX's collectives and lax.ppermute only.
A program may use at most 128 MiB of HBM per device.

v0:
```python
import math

import jax
import jax.numpy as jnp
from jax import lax
from jax.sharding import PartitionSpec as P


def padded(block, sides, width):
    for axis, dim in sides:
        count = lax.axis_size(axis)
        forward = [(i, i + 1) for i in range(count - 1)]
        backward = [(target, source) for source, target in forward]
        low = lax.ppermute(
            lax.slice_in_dim(block, block.shape[dim] - width, None, axis=dim), axis, forward
        )
        high = lax.ppermute(lax.slice_in_dim(block, 0, width, axis=dim), axis, backward)
        block = jnp.concatenate([low, block, high], axis=dim)
    return block


def back_project(grad_flat, point_weight):
    return lax.dot_general(
        grad_flat,
        lax.all_gather(point_weight, ("slide", "row", "col"), axis=0, tiled=True),
        (((1,), (1,)), ((), ())),
        preferred_element_type=jnp.float32,
    ).astype(jnp.bfloat16)


def on_device(features, out_grad, depth_weight, point_weight):
    rows = features.shape[1]
    cols = features.shape[2]
    chans = features.shape[3]
    total = lax.axis_size("slide") * lax.axis_size("row") * lax.axis_size("col") * rows * cols
    scale = 1.0 / math.sqrt(total)
    grad_flat = out_grad[0].reshape(rows * cols, chans)
    feat_pad = padded(features, (("row", 1), ("col", 2)), 2)[0]
    mid_grad = back_project(grad_flat, point_weight).reshape(rows, cols, chans)
    grad_pad = padded(mid_grad[None], (("row", 1), ("col", 2)), 2)[0]
    taps = depth_weight.astype(jnp.float32)
    mid = jnp.zeros((rows, cols, chans), jnp.float32)
    back = jnp.zeros((rows, cols, chans), jnp.float32)
    mid_f = mid_grad.astype(jnp.float32)
    tap_terms = []
    for a in range(3):
        for b in range(3):
            window = feat_pad[2 * a : 2 * a + rows, 2 * b : 2 * b + cols].astype(jnp.float32)
            mid = mid + taps[a * 3 + b] * window
            back = back + taps[a * 3 + b] * grad_pad[
                4 - 2 * a : 4 - 2 * a + rows, 4 - 2 * b : 4 - 2 * b + cols
            ].astype(jnp.float32)
            tap_terms.append(jnp.sum(window * mid_f, axis=(0, 1)))
    mid_flat = mid.astype(jnp.bfloat16).reshape(rows * cols, chans)
    owned = lax.psum_scatter(
        lax.dot_general(
            mid_flat, grad_flat, (((0,), (0,)), ((), ())), preferred_element_type=jnp.float32
        ),
        ("slide", "row", "col"),
        scatter_dimension=0,
        tiled=True,
    )
    depth_grad = lax.psum(jnp.stack(tap_terms), ("slide", "row", "col")) * scale
    feature_grad = back.astype(jnp.bfloat16)[None]
    return (feature_grad, owned * scale, depth_grad)


def solution(mesh):
    placed = (
        P("slide", "row", "col", None),
        P("slide", "row", "col", None),
        P(),
        P(("slide", "row", "col"), None),
    )
    return jax.shard_map(
        on_device,
        mesh=mesh,
        in_specs=placed,
        out_specs=(P("slide", "row", "col", None), P(("slide", "row", "col"), None), P()),
        check_vma=False,
    )
```

profile of v0, /device:TPU:1, one launch (start us, length us, event | category | flops | bytes accessed | tf_op | source)
XLA Modules:
  0.0 971.1 jit_solution(7291026716896225350)
XLA Ops:
  7.2 0.0 copy-start.2
  7.2 0.0 all-reduce.3.cloned.1.call-start
  7.2 1.0 fusion.22
  8.2 0.0 copy-start.3
  8.2 10.2 %collective-permute-start.4 = (bf16[1,2,128,256]{3,2,1,0:T(8,128)(2,1)S(1)}, bf16[1,2,128,256]{3,2,1,0:T(8,128)(2,1)S(1)}, u32[]{:S(2)}, u32[]{:S(2)}) collective-permute-start(bf16[1,2,128,256]{3,2,1,0:T(8,128)(2,1)S(1)} %get-tuple-element.17), channel_id=1, source_target_pairs={{0,4},{4,8},{8,12},{1,5},{5,9},{9,13},{2,6},{6,10},{10,14},{3,7},{... | collective-permute-start | bytes 393224 | tf_op jit(solution)/shard_map/ppermute | solution.py:14
  18.4 1.9 collective-permute-start.5
  20.4 0.0 collective-permute-done.4
  20.4 2.5 constant_dynamic-update-slice_fusion.1
  22.9 5.9 collective-permute-done.5
  28.7 0.0 copy-start.1
  28.8 2.1 copy-done.1
  30.8 0.1 fusion.21
  31.0 4.0 collective-permute-start.6
  34.9 1.3 collective-permute-start.7
  36.2 0.0 copy-done.2
  36.3 0.0 copy-done.3
  36.3 609.1 %all-gather = bf16[256,1,256]{2,1,0:T(2,128)(2,1)S(1)} all-gather(bf16[1,1,256]{2,1,0:T(2,128)(2,1)S(1)} %bitcast.71), channel_id=1, replica_groups=mesh['slide'=16,'row'=4,'col'=4] {'slide','row','col'}, dimensions={0}, use_global_device_ids=true | all-gather | bytes 131584 | tf_op jit(solution)/shard_map/all_gather | solution.py:25
  645.4 0.0 collective-permute-done.6
  645.4 0.0 collective-permute-done.7
  645.4 7.2 maximum_bitcast_fusion.1
  652.6 22.3 %fusion.17 = (f32[256]{0:T(256)S(1)}, f32[256]{0:T(256)S(1)}, f32[256]{0:T(256)S(1)}, f32[256]{0:T(256)S(1)}, f32[256]{0:T(256)S(1)}, /*index=5*/f32[256]{0:T(25...) fusion(bf16[68,132,256]{2,1,0:T(8,128)(2,1)} %maximum_bitcast_fusion.1, ...), kind=kOutput, calls=%fused_computation.36 | convolution fusion | flops 1134556928 | bytes 46277632 | tf_op jit(solution)/shard_map/dot_general | solution.py:23
  674.9 0.0 copy-start
  674.9 22.8 %fusion.8 = bf16[64,128,256]{2,1,0:T(8,128)(2,1)S(1)} fusion(f32[256]{0:T(256)S(1)} %bitcast.69, f32[256]{0:T(256)S(1)} %bitcast.67, f32[256]{0:T(256)S(1)} %bitcast.65, f32[256]{0:T(256)S(1)} %bitcast.63, f32[256]{0:T(256)S(1)} %bitcast.61, f32[256]{0:T(256)S(1)} %bitcast.59, f32[256]{0:T(256)S(1)} %bitcast.57, f32[256]{0:T(256)S(1)} %bitcast.55, ...), kind=kLoop, calls=%fused_computation.27 | loop fusion | flops 56623104 | bytes 41952256 | tf_op jit(solution)/shard_map/convert_element_type | solution.py:54
  697.7 0.0 copy-done
  697.7 2.0 fusion.25
  699.7 0.0 all-reduce.3.cloned.1.call-update
  699.8 79.8 %psum.7 = f32[9,256]{1,0:T(8,128)S(1)} all-reduce(f32[9,256]{1,0:T(8,128)S(1)} %stack.39), channel_id=1, replica_groups=mesh['slide'=16,'row'=4,'col'=4] {'slide','row','col'}, use_global_device_ids=true, to_apply=%region_10.0 | all-reduce | flops 2304 | bytes 18432 | tf_op jit(solution)/shard_map/psum | solution.py:63
  779.5 1.0 fusion.23
  780.5 3.8 collective-permute-start
  784.3 1.9 collective-permute-start.1
  786.2 0.6 broadcast_multiply_fusion
  786.8 0.0 collective-permute-done
  786.9 8.0 collective-permute-done.1
  794.8 1.1 pad_maximum_fusion.2
  796.0 2.8 collective-permute-start.2
  798.8 1.3 collective-permute-start.3
  800.1 147.7 %all-reduce.3.cloned.1.call-done = f32[256,256]{1,0:T(8,128)} async-done(((f32[256,256]{1,0:T(8,128)}), f32[256,256]{1,0:T(8,128)}) %all-reduce.3.cloned.1.call-update) | async-done | bytes 262160
  947.8 1.3 dynamic-slice_multiply_fusion
  949.1 0.0 collective-permute-done.2
  949.1 0.0 collective-permute-done.3
  949.1 4.2 maximum_bitcast_fusion
  953.3 10.9 %fusion.18 = bf16[1,64,128,256]{3,2,1,0:T(8,128)(2,1)} fusion(bf16[68,132,256]{2,1,0:T(8,128)(2,1)S(1)} %maximum_bitcast_fusion, f32[256]{0:T(256)S(1)} %bitcast.70, f32[256]{0:T(256)S(1)} %bitcast.68, f32[256]{0:T(256)S(1)} %bitcast.66, f32[256]{0:T(256)S(1)} %bitcast.64, f32[256]{0:T(256)S(1)} %bitcast.62, f32[256]{0:T(256)S(1)} %bitcast.60, ...), kind=kLoop, calls=%fused_computation.40 | loop fusion | flops 56623104 | bytes 41952256 | tf_op jit(solution)/shard_map/broadcast_in_dim | solution.py:64
  (4 shorter events, 0.1 us)
Async XLA Ops:
  7.2 29.1 %copy-start.2 = (bf16[9,256]{1,0:T(8,128)(2,1)S(1)}, bf16[9,256]{1,0:T(8,128)(2,1)}, u32[]{:S(2)}) copy-start(bf16[9,256]{1,0:T(8,128)(2,1)} %param.6) | copy-start | bytes 13828
  7.2 940.7 %all-reduce.3.cloned.1.call-start = ((), (), s32[]{:S(2)}) async-start(), calls=%async_computation | async-start | bytes 524288
  8.2 28.0 %copy-start.3 = (bf16[1,256]{1,0:T(2,128)(2,1)S(1)}, bf16[1,256]{1,0:T(2,128)(2,1)}, u32[]{:S(2)}) copy-start(bf16[1,256]{1,0:T(2,128)(2,1)} %param.7) | copy-start | bytes 1540
  8.2 12.1 %collective-permute-start.4 = (bf16[1,2,128,256]{3,2,1,0:T(8,128)(2,1)S(1)}, bf16[1,2,128,256]{3,2,1,0:T(8,128)(2,1)S(1)}, u32[]{:S(2)}, u32[]{:S(2)}) collective-permute-start(bf16[1,2,128,256]{3,2,1,0:T(8,128)(2,1)S(1)} %get-tuple-element.17), channel_id=1, source_target_pairs={{0,4},{4,8},{8,12},{1,5},{5,9},{9,13},{2,6},{6,10},{10,14},{3,7},{... | collective-permute-start | bytes 393224 | tf_op jit(solution)/shard_map/ppermute | solution.py:14
  18.4 10.3 %collective-permute-start.5 = (bf16[1,2,128,256]{3,2,1,0:T(8,128)(2,1)S(1)}, bf16[1,2,128,256]{3,2,1,0:T(8,128)(2,1)S(1)}, u32[]{:S(2)}, u32[]{:S(2)}) collective-permute-start(bf16[1,2,128,256]{3,2,1,0:T(8,128)(2,1)S(1)} %get-tuple-element.16), channel_id=1, source_target_pairs={{4,0},{8,4},{12,8},{5,1},{9,5},{13,9},{6,2},{10,6},{14,10},{7,3},{... | collective-permute-start | bytes 393224 | tf_op jit(solution)/shard_map/ppermute | solution.py:17
  28.7 2.1 copy-start.1
  31.0 614.4 %collective-permute-start.6 = (bf16[1,68,2,256]{3,2,1,0:T(2,128)(2,1)S(1)}, bf16[1,68,2,256]{3,2,1,0:T(2,128)(2,1)S(1)}, u32[]{:S(2)}, u32[]{:S(2)}) collective-permute-start(bf16[1,68,2,256]{3,2,1,0:T(2,128)(2,1)S(1)} %get-tuple-element.12), channel_id=1, source_target_pairs={{0,1},{1,2},{2,3},{4,5},{5,6},{6,7},{8,9},{9,10},{10,11},{12,13},{... | collective-permute-start | bytes 208904 | tf_op jit(solution)/shard_map/ppermute | solution.py:14
  34.9 610.4 %collective-permute-start.7 = (bf16[1,68,2,256]{3,2,1,0:T(2,128)(2,1)S(1)}, bf16[1,68,2,256]{3,2,1,0:T(2,128)(2,1)S(1)}, u32[]{:S(2)}, u32[]{:S(2)}) collective-permute-start(bf16[1,68,2,256]{3,2,1,0:T(2,128)(2,1)S(1)} %get-tuple-element.13), channel_id=1, source_target_pairs={{1,0},{2,1},{3,2},{5,4},{6,5},{7,6},{9,8},{10,9},{11,10},{13,12},{... | collective-permute-start | bytes 208904 | tf_op jit(solution)/shard_map/ppermute | solution.py:17
  674.9 22.8 %copy-start = (bf16[1,64,128,256]{3,2,1,0:T(8,128)(2,1)S(1)}, bf16[1,64,128,256]{3,2,1,0:T(8,128)(2,1)}, u32[]{:S(2)}) copy-start(bf16[1,64,128,256]{3,2,1,0:T(8,128)(2,1)} %param.5) | copy-start | bytes 12582916
  780.5 6.3 collective-permute-start
  784.3 10.5 %collective-permute-start.1 = (bf16[1,2,128,256]{3,2,1,0:T(8,128)(2,1)S(1)}, bf16[1,2,128,256]{3,2,1,0:T(8,128)(2,1)S(1)}, u32[]{:S(2)}, u32[]{:S(2)}) collective-permute-start(bf16[1,2,128,256]{3,2,1,0:T(8,128)(2,1)S(1)} %get-tuple-element.19), channel_id=1, source_target_pairs={{4,0},{8,4},{12,8},{5,1},{9,5},{13,9},{6,2},{10,6},{14,10},{7,3},{... | collective-permute-start | bytes 393224 | tf_op jit(solution)/shard_map/ppermute | solution.py:17
  796.0 153.1 %collective-permute-start.2 = (bf16[1,68,2,256]{3,2,1,0:T(2,128)(2,1)S(1)}, bf16[1,68,2,256]{3,2,1,0:T(2,128)(2,1)S(1)}, u32[]{:S(2)}, u32[]{:S(2)}) collective-permute-start(bf16[1,68,2,256]{3,2,1,0:T(2,128)(2,1)S(1)} %get-tuple-element.14), channel_id=1, source_target_pairs={{0,1},{1,2},{2,3},{4,5},{5,6},{6,7},{8,9},{9,10},{10,11},{12,13},{... | collective-permute-start | bytes 208904 | tf_op jit(solution)/shard_map/ppermute | solution.py:14
  798.8 150.3 %collective-permute-start.3 = (bf16[1,68,2,256]{3,2,1,0:T(2,128)(2,1)S(1)}, bf16[1,68,2,256]{3,2,1,0:T(2,128)(2,1)S(1)}, u32[]{:S(2)}, u32[]{:S(2)}) collective-permute-start(bf16[1,68,2,256]{3,2,1,0:T(2,128)(2,1)S(1)} %get-tuple-element.15), channel_id=1, source_target_pairs={{1,0},{2,1},{3,2},{5,4},{6,5},{7,6},{9,8},{10,9},{11,10},{13,12},{... | collective-permute-start | bytes 208904 | tf_op jit(solution)/shard_map/ppermute | solution.py:17
Sparse Core Ops, SparseCore 0:
  699.8 247.9 all-reduce.2
where the time goes:
time: 972 us; the launch traced here: 971 us
  blocking collectives  689 us (71%)
  waiting for transfers between devices  162 us (17%)
  other arithmetic  48.2 us (5%)
  starting transfers between devices  27.2 us (3%)
  matrix products  24.3 us (2%)
  between operations  14.2 us (1%)
    all_gather x1, blocking collectives, back_project(): lax.all_gather(point_weight, ('slide', 'row', 'col'), axis=0, tiled=True)  609 us
    unnamed x2, waiting for transfers between devices  148 us
    psum x1, blocking collectives, on_device(): depth_grad = lax.psum(jnp.stack(tap_terms), ('slide', 'row', 'col')) * scale  79.8 us
    convert_element_type x1, other arithmetic, on_device(): mid_flat = mid.astype(jnp.bfloat16).reshape(rows * cols, chans)  22.8 us
    dot_general x1, matrix products, back_project(): lax.dot_general(grad_flat, lax.all_gather(point_weight, ('slide', 'row',...  22.3 us
    ppermute x4, starting transfers between devices, padded(): lax.ppermute(lax.slice_in_dim(block, block.shape[dim] - width, None, axis...  20.8 us
  transfers between devices with their start and end apart: 9, of which 3 were waited for; matrix products, arithmetic and copies ran while one was open for 1% of the time, Pallas kernels for 0%

commit v1 on v0

v1 whole, which is shorter than its diff:
```python
import math

import jax
import jax.numpy as jnp
from jax import lax
from jax.experimental import pallas as pl
from jax.experimental.pallas import tpu as pltpu
from jax.sharding import PartitionSpec as P

BF16 = jnp.bfloat16
F32 = jnp.float32
IN_VMEM = pl.BlockSpec(memory_space=pltpu.VMEM)


def whole(body, outs, args, name, flops, limit, scratch=()):
    size = sum(math.prod(x.shape) * x.dtype.itemsize for x in (*args, *outs))
    return pl.pallas_call(
        body,
        out_shape=outs,
        in_specs=[IN_VMEM] * len(args),
        out_specs=[IN_VMEM] * len(outs),
        scratch_shapes=scratch,
        name=name,
        cost_estimate=pl.CostEstimate(
            flops=flops, bytes_accessed=size, transcendentals=0
        ),
        compiler_params=pltpu.CompilerParams(vmem_limit_bytes=limit << 20),
    )(*args)


def shifted(above, grad, below, left, right, out):
    rows, cols, chans = grad.shape

    def put(i, row):
        out[i, :, 0:chans] = jnp.concatenate([row[2:], right[i]], axis=0)
        out[i, :, chans : 2 * chans] = row
        out[i, :, 2 * chans : 3 * chans] = jnp.concatenate(
            [left[i], row[: cols - 2]], axis=0
        )

    for i in range(2):
        put(i, above[i])
        put(rows + 2 + i, below[i])
    lax.fori_loop(0, rows, lambda i, c: (put(i + 2, grad[i]), c)[1], 0)


def moments(feat, above, grad, below, left, right, moment, wide):
    rows, cols, chans = feat.shape
    step = 8
    shifted(above, grad, below, left, right, wide)
    moment[...] = jnp.zeros_like(moment)

    def body(t, c):
        first = pl.multiple_of(t * step, step)
        lhs = feat[pl.ds(first, step)].reshape(step * cols, chans)
        for a in range(3):
            rhs = wide[pl.ds(first + 4 - 2 * a, step)]
            moment[a] += lax.dot_general(
                lhs,
                rhs.reshape(step * cols, 3 * chans),
                (((0,), (0,)), ((), ())),
                preferred_element_type=F32,
            )
        return c

    lax.fori_loop(0, rows // step, body, 0)


def finish(moment, point, taps, out):
    chans = point.shape[0]
    p = point[...].astype(F32)
    acc = jnp.zeros((chans, chans), F32)
    lane = lax.broadcasted_iota(jnp.int32, (chans, 128), 1)
    sums = jnp.zeros((chans, 128), F32)
    for a in range(3):
        for b in range(3):
            k = 3 * a + b
            m = moment[a, :, b * chans : (b + 1) * chans]
            acc = acc + taps[:, k : k + 1] * m
            sums = jnp.where(lane == k, jnp.sum(p * m, axis=1, keepdims=True), sums)
    groups = out.shape[0]
    share = chans // groups
    tap_rows = sums.T[:16]
    for s in range(groups):
        out[s, :share] = acc[s * share : (s + 1) * share]
        out[s, share:] = tap_rows


def second(got, out):
    total = got[0]
    for s in range(1, got.shape[0]):
        total = total + got[s]
    rows = total.shape[0] // 2
    tap = total[rows:]
    sub = lax.broadcasted_iota(jnp.int32, tap.shape, 0)
    for r in range(out.shape[0]):
        out[r] = jnp.where(sub == 9, total[r : r + 1], tap)


def third(scale, got, taps, row):
    total = got[0]
    for s in range(1, got.shape[0]):
        total = total + got[s]
    total = total * scale
    taps[...] = total[:9]
    row[...] = total[9:10]


def back(above, grad, below, left, right, point, taps, out, wide, weights):
    rows, cols, chans = grad.shape
    step = 8
    p = point[...].astype(F32)
    for k in range(9):
        weights[k // 3, :, (k % 3) * chans : (k % 3 + 1) * chans] = (
            p * taps[:, k : k + 1]
        ).astype(BF16)
    shifted(above, grad, below, left, right, wide)

    def body(t, c):
        first = pl.multiple_of(t * step, step)
        acc = jnp.zeros((step * cols, chans), F32)
        for a in range(3):
            lhs = wide[pl.ds(first + 4 - 2 * a, step)]
            acc = acc + lax.dot_general(
                lhs.reshape(step * cols, 3 * chans),
                weights[a],
                (((1,), (1,)), ((), ())),
                preferred_element_type=F32,
            )
        out[pl.ds(first, step)] = acc.reshape(step, cols, chans).astype(BF16)
        return c

    lax.fori_loop(0, rows // step, body, 0)


def spread(x, axes):
    count = lax.axis_size(axes)
    return lax.all_to_all(
        jnp.broadcast_to(x[None], (count, *x.shape)), axes, 0, 0, tiled=True
    )


def moved(x, axis, by):
    count = lax.axis_size(axis)
    pairs = [(i, i + by) for i in range(count) if 0 <= i + by < count]
    return lax.ppermute(x, axis, pairs)


def on_device(features, out_grad, depth_weight, point_weight):
    feat, grad = features[0], out_grad[0]
    rows, cols, chans = feat.shape
    place = ("row", "col")
    slides = lax.axis_size("slide")
    scale = 1.0 / math.sqrt(slides * lax.axis_size(place) * rows * cols)
    taps = depth_weight.astype(F32).T

    above = moved(grad[rows - 2 :], "row", 1)
    below = moved(grad[:2], "row", -1)
    block = spread(point_weight, place).reshape(-1, chans)
    ends = [
        jnp.concatenate([x[:, s] for x in (above, grad, below)], axis=0)
        for s in (slice(cols - 2, None), slice(0, 2))
    ]
    left = moved(ends[0], "col", 1)
    right = moved(ends[1], "col", -1)
    point = spread(block, "slide").reshape(-1, chans)

    halo = (above, grad, below, left, right)
    macs = rows * cols * chans * chans
    wide = pltpu.VMEM((rows + 4, cols, 3 * chans), BF16)
    (moment,) = whole(
        moments,
        [jax.ShapeDtypeStruct((3, chans, 3 * chans), F32)],
        (feat, *halo),
        "moments",
        18 * macs,
        56,
        [wide],
    )
    (parts,) = whole(
        finish,
        [jax.ShapeDtypeStruct((slides, 32, chans), F32)],
        (moment, point, taps),
        "finish",
        36 * chans * chans,
        32,
    )
    got = lax.all_to_all(parts, "slide", 0, 0, tiled=True)
    (feature_grad,) = whole(
        back,
        [jax.ShapeDtypeStruct((rows, cols, chans), BF16)],
        (*halo, point, taps),
        "back",
        18 * macs,
        56,
        [wide, pltpu.VMEM((3, chans, 3 * chans), BF16)],
    )
    (parts,) = whole(
        second,
        [jax.ShapeDtypeStruct((lax.axis_size(place), 16, chans), F32)],
        (got,),
        "second",
        1 << 20,
        16,
    )
    got = lax.all_to_all(parts, place, 0, 0, tiled=True)
    depth_grad, point_grad = whole(
        lambda *refs: third(scale, *refs),
        [jax.ShapeDtypeStruct((9, chans), F32), jax.ShapeDtypeStruct((1, chans), F32)],
        (got,),
        "third",
        1 << 20,
        16,
    )
    return feature_grad[None], point_grad, depth_grad


def solution(mesh):
    placed = (
        P("slide", "row", "col", None),
        P("slide", "row", "col", None),
        P(),
        P(("slide", "row", "col"), None),
    )
    return jax.shard_map(
        on_device,
        mesh=mesh,
        in_specs=placed,
        out_specs=(P("slide", "row", "col", None), P(("slide", "row", "col"), None), P()),
        check_vma=False,
    )
```

time: 972 us -> 111 us (0.11)
  blocking collectives: 689 us -> 16.6 us
  waiting for transfers between devices: 162 us -> 7.02 us
  other arithmetic: 48.2 us -> 1.6 us
  Pallas kernels: 0 us -> 37.7 us
  matrix products: 24.3 us -> 0 us
  between operations: 14.2 us -> 0.81 us
  starting transfers between devices: 27.2 us -> 39.4 us
    all_gather x1 -> x0, blocking collectives: 609 us -> none  [back_project(): lax.all_gather(point_weight, ('slide', 'row', 'col'), axis=0, tiled=True)]
    unnamed x2 -> x0, waiting for transfers between devices: 148 us -> none
    psum x1 -> x0, blocking collectives: 79.8 us -> none  [on_device(): depth_grad = lax.psum(jnp.stack(tap_terms), ('slide', 'row', 'col')) * scale]
    pallas_call x0 -> x5, Pallas kernels: none -> 37.7 us  [whole(): pl.pallas_call(body, out_shape=outs, in_specs=[IN_VMEM] * len(args), out_...]
    dot_general x2 -> x0, matrix products: 24.3 us -> none  [the longest x1 22.3 us: back_project(): lax.dot_general(grad_flat, lax.all_gather(point_weight, ('slide', 'row',...]
    all_to_all x0 -> x3, starting transfers between devices: none -> 23.5 us  [the longest x2 17.8 us: spread(): lax.all_to_all(jnp.broadcast_to(x[None], (count, *x.shape)), axes, 0, 0,...]
    convert_element_type x1 -> x0, other arithmetic: 22.8 us -> none  [on_device(): mid_flat = mid.astype(jnp.bfloat16).reshape(rows * cols, chans)]
    all_to_all x0 -> x1, blocking collectives: none -> 16.6 us  [on_device(): got = lax.all_to_all(parts, 'slide', 0, 0, tiled=True)]
  transfers between devices with their start and end apart: 9 -> 7, of which waited for: 3 -> 2; matrix products, arithmetic and copies ran while one was open for 1% -> 5% of each run, Pallas kernels for 0% -> 32%
where the time goes in v1:
time: 111 us; the launch traced here: 110 us
  starting transfers between devices  39.4 us (35%)
  Pallas kernels  37.7 us (34%)
  blocking collectives  16.6 us (15%)
  local copies, waits for them, and re-layouts  7.11 us (6%)
  waiting for transfers between devices  7.02 us (6%)
  other arithmetic  1.6 us (1%)
    pallas_call x5, Pallas kernels, whole(): pl.pallas_call(body, out_shape=outs, in_specs=[IN_VMEM] * len(args), out_...  37.7 us
    all_to_all x2, starting transfers between devices, spread(): lax.all_to_all(jnp.broadcast_to(x[None], (count, *x.shape)), axes, 0, 0,...  17.8 us
    all_to_all x1, blocking collectives, on_device(): got = lax.all_to_all(parts, 'slide', 0, 0, tiled=True)  16.6 us
    ppermute x4, starting transfers between devices, moved(): return lax.ppermute(x, axis, pairs)  15.9 us
    all_to_all x2, waiting for transfers between devices, spread(): lax.all_to_all(jnp.broadcast_to(x[None], (count, *x.shape)), axes, 0, 0,...  6.08 us
    all_to_all x1, starting transfers between devices, on_device(): got = lax.all_to_all(parts, place, 0, 0, tiled=True)  5.7 us
    unnamed x17, local copies, waits for them, and re-layouts  2.96 us
  transfers between devices with their start and end apart: 7, of which 2 were waited for; matrix products, arithmetic and copies ran while one was open for 5% of the time, Pallas kernels for 32%

profile of v1, /device:TPU:1, one launch (start us, length us, event | category | flops | bytes accessed | tf_op | source)
XLA Modules:
  0.0 110.2 jit_solution(13793034848766114573)
XLA Ops:
  0.6 1.0 slice_bitcast_fusion
  1.6 5.1 %collective-permute-start.1 = (bf16[2,128,256]{2,1,0:T(8,128)(2,1)S(1)}, bf16[2,128,256]{2,1,0:T(8,128)(2,1)S(1)}, u32[]{:S(2)}, u32[]{:S(2)}) collective-permute-start(bf16[2,128,256]{2,1,0:T(8,128)(2,1)S(1)} %get-tuple-element.9), channel_id=1, source_target_pairs={{4,0},{8,4},{12,8},{5,1},{9,5},{13,9},{6,2},{10,6},{14,10},{7,3},{... | collective-permute-start | bytes 393224 | tf_op jit(solution)/shard_map/ppermute | solution.py:146
  6.8 7.0 %collective-permute-start = (bf16[2,128,256]{2,1,0:T(8,128)(2,1)S(1)}, bf16[2,128,256]{2,1,0:T(8,128)(2,1)S(1)}, u32[]{:S(2)}, u32[]{:S(2)}) collective-permute-start(bf16[2,128,256]{2,1,0:T(8,128)(2,1)S(1)} %get-tuple-element.10), channel_id=1, source_target_pairs={{0,4},{4,8},{8,12},{1,5},{5,9},{9,13},{2,6},{6,10},{10,14},{3,7},{... | collective-permute-start | bytes 393224 | tf_op jit(solution)/shard_map/ppermute | solution.py:146
  13.8 1.1 %fusion = (bf16[64,2,256]{2,1,0:T(2,128)(2,1)S(1)}, bf16[64,2,256]{2,1,0:T(2,128)(2,1)S(1)}) fusion(bf16[64,128,256]{2,1,0:T(8,128)(2,1)} %bitcast.16), kind=kLoop, calls=%fused_computation.5 | loop fusion | bytes 262144 | tf_op jit(solution)/shard_map/slice | solution.py:161
  14.9 0.0 collective-permute-done.1.below
  14.9 0.0 copy-start.3
  14.9 0.9 collective-permute-done.above
  15.9 0.0 copy-start.4
  15.9 0.1 pad_maximum_fusion
  16.0 2.5 %collective-permute-start.2 = (bf16[68,2,256]{2,1,0:T(2,128)(2,1)S(1)}, bf16[68,2,256]{2,1,0:T(2,128)(2,1)S(1)}, u32[]{:S(2)}, u32[]{:S(2)}) collective-permute-start(bf16[68,2,256]{2,1,0:T(2,128)(2,1)S(1)} %pad_maximum_fusion), channel_id=1, source_target_pairs={{0,1},{1,2},{2,3},{4,5},{5,6},{6,7},{8,9},{9,10},{10,11},{12,13},{... | collective-permute-start | bytes 208904 | tf_op jit(solution)/shard_map/ppermute | solution.py:146
  18.5 0.1 pad_maximum_fusion.1
  18.6 1.3 %collective-permute-start.3 = (bf16[68,2,256]{2,1,0:T(2,128)(2,1)S(1)}, bf16[68,2,256]{2,1,0:T(2,128)(2,1)S(1)}, u32[]{:S(2)}, u32[]{:S(2)}) collective-permute-start(bf16[68,2,256]{2,1,0:T(2,128)(2,1)S(1)} %pad_maximum_fusion.1), channel_id=1, source_target_pairs={{1,0},{2,1},{3,2},{5,4},{6,5},{7,6},{9,8},{10,9},{11,10},{13,12},{... | collective-permute-start | bytes 208904 | tf_op jit(solution)/shard_map/ppermute | solution.py:146
  19.9 0.7 reduce
  20.6 0.5 broadcast.2
  21.1 0.7 reduce.1
  21.8 0.6 reshape.17
  22.4 11.0 %all-to-all-start = ((bf16[16,2,128]{2,1,0:T(2,128)(2,1)}), bf16[16,2,128]{2,1,0:T(2,128)(2,1)S(1)}, u32[]{:S(2)}, u32[]{:S(2)}) async-start(bf16[16,2,128]{2,1,0:T(2,128)(2,1)} %reshape.17), calls=%async_computation | async-start | bytes 16384 | tf_op jit(solution)/shard_map/all_to_all | solution.py:138
  33.4 0.8 copy.9
  34.3 0.0 copy-start.1
  34.3 6.1 %all-to-all-done = bf16[16,2,128]{2,1,0:T(2,128)(2,1)S(1)} async-done(((bf16[16,2,128]{2,1,0:T(2,128)(2,1)}), bf16[16,2,128]{2,1,0:T(2,128)(2,1)S(1)}, u32[]{:S(2)}, u32[]{:S(2)}) %all-to-all-start) | async-done | bytes 8224 | tf_op jit(solution)/shard_map/all_to_all | solution.py:138
  40.4 0.7 broadcast_in_dim.21
  41.0 6.8 %all-to-all-start.1 = ((bf16[16,16,256]{2,1,0:T(8,128)(2,1)}), bf16[16,16,256]{2,1,0:T(8,128)(2,1)S(1)}, u32[]{:S(2)}, u32[]{:S(2)}) async-start(bf16[16,16,256]{2,1,0:T(8,128)(2,1)} %broadcast_in_dim.21), calls=%async_computation.1 | async-start | bytes 262144 | tf_op jit(solution)/shard_map/all_to_all | solution.py:138
  47.8 0.0 collective-permute-done.2.left
  47.8 0.0 copy-start.5
  47.8 0.0 collective-permute-done.3.right
  47.8 0.0 copy-start.6
  47.8 0.0 copy-done.3
  47.9 0.0 copy-done.4
  47.9 0.6 copy-done.5
  48.5 0.0 copy-done.6
  48.5 17.9 %moments.1.moment = f32[3,256,768]{2,1,0:T(8,128)} custom-call(bf16[64,128,256]{2,1,0:T(8,128)(2,1)} %bitcast.20, bf16[2,128,256]{2,1,0:T(8,128)(2,1)} %copy-done.4, bf16[64,128,256]{2,1,0:T(8,128)(2,1)} %bitcast.17, bf16[2,128,256]{2,1,0:T(8,128)(2,1)} %copy-done.3, bf16[68,2,256]{2,1,0:T(2,128)(2,1)} %copy-done.5, bf16[68,2,256]{2,1,0:T(2,128)(2,1)} %copy-done.6), custom_call_target="tpu_custom_call" | custom-call | flops 9663676416 | bytes 11149312 | tf_op jit(solution)/shard_map/moments/pallas_call | solution.py:17
  66.4 0.0 all-to-all-done.1
  66.4 0.0 copy-start.2
  66.4 0.0 copy-done.1
  66.4 0.0 copy-start
  66.4 1.7 %copy-done = f32[3,256,768]{2,1,0:T(8,128)S(1)} copy-done((f32[3,256,768]{2,1,0:T(8,128)S(1)}, f32[3,256,768]{2,1,0:T(8,128)}, u32[]{:S(2)}) %copy-start) | copy-done | bytes 2359320
  68.1 1.1 finish.1
  69.2 16.6 %all_to_all.20.got = f32[16,32,256]{2,1,0:T(8,128)S(1)} all-to-all(f32[16,32,256]{2,1,0:T(8,128)S(1)} %finish.1), channel_id=1, replica_groups=mesh['slide'=16,'row'=4,'col'=4] {'slide'}, dimensions={0} | all-to-all | bytes 1048576 | tf_op jit(solution)/shard_map/all_to_all | solution.py:188
  85.8 0.7 second.1
  86.5 5.7 %all-to-all-start.3 = ((f32[16,16,256]{2,1,0:T(8,128)}), f32[16,16,256]{2,1,0:T(8,128)S(1)}, u32[]{:S(2)}, u32[]{:S(2)}) async-start(f32[16,16,256]{2,1,0:T(8,128)} %second.1), calls=%async_computation.3 | async-start | bytes 524288 | tf_op jit(solution)/shard_map/all_to_all | solution.py:206
  92.2 0.0 copy-done.2
  92.2 17.3 %back.1 = bf16[64,128,256]{2,1,0:T(8,128)(2,1)} custom-call(bf16[2,128,256]{2,1,0:T(8,128)(2,1)} %copy-done.4, bf16[64,128,256]{2,1,0:T(8,128)(2,1)} %bitcast.18, bf16[2,128,256]{2,1,0:T(8,128)(2,1)} %copy-done.3, bf16[68,2,256]{2,1,0:T(2,128)(2,1)} %copy-done.5, bf16[68,2,256]{2,1,0:T(2,128)(2,1)} %copy-done.6, bf16[256,256]{1,0:T(8,128)(2,1)} %bitcast.15, ...), custom_call_target="tpu_custom_call" | custom-call | flops 9663676416 | bytes 8930304 | tf_op jit(solution)/shard_map/back/pallas_call | solution.py:17
  109.6 0.0 all-to-all-done.3.refs_0_
  109.6 0.6 third.1
  (5 shorter events, 0.0 us)
Async XLA Ops:
  1.6 13.3 %collective-permute-start.1 = (bf16[2,128,256]{2,1,0:T(8,128)(2,1)S(1)}, bf16[2,128,256]{2,1,0:T(8,128)(2,1)S(1)}, u32[]{:S(2)}, u32[]{:S(2)}) collective-permute-start(bf16[2,128,256]{2,1,0:T(8,128)(2,1)S(1)} %get-tuple-element.9), channel_id=1, source_target_pairs={{4,0},{8,4},{12,8},{5,1},{9,5},{13,9},{6,2},{10,6},{14,10},{7,3},{... | collective-permute-start | bytes 393224 | tf_op jit(solution)/shard_map/ppermute | solution.py:146
  6.8 9.1 %collective-permute-start = (bf16[2,128,256]{2,1,0:T(8,128)(2,1)S(1)}, bf16[2,128,256]{2,1,0:T(8,128)(2,1)S(1)}, u32[]{:S(2)}, u32[]{:S(2)}) collective-permute-start(bf16[2,128,256]{2,1,0:T(8,128)(2,1)S(1)} %get-tuple-element.10), channel_id=1, source_target_pairs={{0,4},{4,8},{8,12},{1,5},{5,9},{9,13},{2,6},{6,10},{10,14},{3,7},{... | collective-permute-start | bytes 393224 | tf_op jit(solution)/shard_map/ppermute | solution.py:146
  14.9 32.9 %copy-start.3 = (bf16[2,128,256]{2,1,0:T(8,128)(2,1)}, bf16[2,128,256]{2,1,0:T(8,128)(2,1)S(1)}, u32[]{:S(2)}) copy-start(bf16[2,128,256]{2,1,0:T(8,128)(2,1)S(1)} %collective-permute-done.1.below) | copy-start | bytes 393220
  15.9 32.0 %copy-start.4 = (bf16[2,128,256]{2,1,0:T(8,128)(2,1)}, bf16[2,128,256]{2,1,0:T(8,128)(2,1)S(1)}, u32[]{:S(2)}) copy-start(bf16[2,128,256]{2,1,0:T(8,128)(2,1)S(1)} %collective-permute-done.above) | copy-start | bytes 393220
  16.0 31.8 %collective-permute-start.2 = (bf16[68,2,256]{2,1,0:T(2,128)(2,1)S(1)}, bf16[68,2,256]{2,1,0:T(2,128)(2,1)S(1)}, u32[]{:S(2)}, u32[]{:S(2)}) collective-permute-start(bf16[68,2,256]{2,1,0:T(2,128)(2,1)S(1)} %pad_maximum_fusion), channel_id=1, source_target_pairs={{0,1},{1,2},{2,3},{4,5},{5,6},{6,7},{8,9},{9,10},{10,11},{12,13},{... | collective-permute-start | bytes 208904 | tf_op jit(solution)/shard_map/ppermute | solution.py:146
  18.6 29.2 %collective-permute-start.3 = (bf16[68,2,256]{2,1,0:T(2,128)(2,1)S(1)}, bf16[68,2,256]{2,1,0:T(2,128)(2,1)S(1)}, u32[]{:S(2)}, u32[]{:S(2)}) collective-permute-start(bf16[68,2,256]{2,1,0:T(2,128)(2,1)S(1)} %pad_maximum_fusion.1), channel_id=1, source_target_pairs={{1,0},{2,1},{3,2},{5,4},{6,5},{7,6},{9,8},{10,9},{11,10},{13,12},{... | collective-permute-start | bytes 208904 | tf_op jit(solution)/shard_map/ppermute | solution.py:146
  22.4 17.9 %all-to-all-start = ((bf16[16,2,128]{2,1,0:T(2,128)(2,1)}), bf16[16,2,128]{2,1,0:T(2,128)(2,1)S(1)}, u32[]{:S(2)}, u32[]{:S(2)}) async-start(bf16[16,2,128]{2,1,0:T(2,128)(2,1)} %reshape.17), calls=%async_computation | async-start | bytes 16384 | tf_op jit(solution)/shard_map/all_to_all | solution.py:138
  34.3 32.2 %copy-start.1 = (f32[9,256]{0,1:T(8,128)}, f32[9,256]{0,1:T(8,128)S(1)}, u32[]{:S(2)}) copy-start(f32[9,256]{0,1:T(8,128)S(1)} %copy.9) | copy-start | bytes 27652
  41.0 25.4 %all-to-all-start.1 = ((bf16[16,16,256]{2,1,0:T(8,128)(2,1)}), bf16[16,16,256]{2,1,0:T(8,128)(2,1)S(1)}, u32[]{:S(2)}, u32[]{:S(2)}) async-start(bf16[16,16,256]{2,1,0:T(8,128)(2,1)} %broadcast_in_dim.21), calls=%async_computation.1 | async-start | bytes 262144 | tf_op jit(solution)/shard_map/all_to_all | solution.py:138
  47.8 0.6 copy-start.5
  47.8 0.6 copy-start.6
  66.4 25.8 %copy-start.2 = (bf16[16,16,256]{2,1,0:T(8,128)(2,1)}, bf16[16,16,256]{2,1,0:T(8,128)(2,1)S(1)}, u32[]{:S(2)}) copy-start(bf16[16,16,256]{2,1,0:T(8,128)(2,1)S(1)} %all-to-all-done.1) | copy-start | bytes 393220
  66.4 1.7 %copy-start = (f32[3,256,768]{2,1,0:T(8,128)S(1)}, f32[3,256,768]{2,1,0:T(8,128)}, u32[]{:S(2)}) copy-start(f32[3,256,768]{2,1,0:T(8,128)} %moments.1.moment) | copy-start | bytes 7077892
  86.5 23.0 %all-to-all-start.3 = ((f32[16,16,256]{2,1,0:T(8,128)}), f32[16,16,256]{2,1,0:T(8,128)S(1)}, u32[]{:S(2)}, u32[]{:S(2)}) async-start(f32[16,16,256]{2,1,0:T(8,128)} %second.1), calls=%async_computation.3 | async-start | bytes 524288 | tf_op jit(solution)/shard_map/all_to_all | solution.py:206

commit v2 on v1

v2 whole, which is shorter than its diff:
```python
import functools
import math

import jax
import jax.numpy as jnp
from jax import lax
from jax.experimental import pallas as pl
from jax.experimental.pallas import tpu as pltpu
from jax.sharding import PartitionSpec as P

BF16 = jnp.bfloat16
F32 = jnp.float32
IN_VMEM = pl.BlockSpec(memory_space=pltpu.VMEM)


def whole(body, outs, args, name, flops, limit, scratch=(), specs=None, alias=None):
    size = sum(math.prod(x.shape) * x.dtype.itemsize for x in (*args, *outs))
    ins, outs_at = specs or ([IN_VMEM] * len(args), [IN_VMEM] * len(outs))
    return pl.pallas_call(
        body,
        out_shape=outs,
        in_specs=ins,
        out_specs=outs_at,
        scratch_shapes=scratch,
        name=name,
        input_output_aliases=alias or {},
        cost_estimate=pl.CostEstimate(
            flops=flops, bytes_accessed=size, transcendentals=0
        ),
        compiler_params=pltpu.CompilerParams(vmem_limit_bytes=limit << 20),
    )(*args)


def prepare(row, grad, rows_out, top, bottom, lo, hi, first, last, sems):
    rows, cols, _ = grad.shape
    copies = [
        pltpu.make_async_copy(a, b, sems.at[n])
        for n, (a, b) in enumerate(
            (
                (grad.at[:, pl.ds(0, 8)], first),
                (grad.at[:, pl.ds(cols - 8, 8)], last),
                (grad.at[pl.ds(0, 2)], top),
                (grad.at[pl.ds(rows - 2, 2)], bottom),
            )
        )
    ]
    for copy in copies:
        copy.start()
    half = row.shape[1] // 2
    r = row[...].astype(F32)
    two = jnp.concatenate([r[:, :half], r[:, half:]], axis=0).astype(BF16)
    rows_out[...] = jnp.broadcast_to(two[None], rows_out.shape)
    for copy in copies:
        copy.wait()
    lo[...] = first[:, :2]
    hi[...] = last[:, 6:]


def ends(top, bottom, left, right, top_out, bottom_out):
    rows = left.shape[0]
    cols = top.shape[1]
    for out, part, at in ((top_out, top, 0), (bottom_out, bottom, rows - 2)):
        out[:, :cols] = part[...]
        fill = jnp.zeros((2, 4, left.shape[2]), BF16)
        out[:, cols:] = jnp.concatenate(
            [left[at : at + 2], right[at : at + 2], fill], axis=1
        )


def fetch(source, target, sems, bounds, offset):
    copies = [
        pltpu.make_async_copy(
            source.at[pl.ds(low, high - low)],
            target.at[pl.ds(low + offset, high - low)],
            sems.at[n],
        )
        for n, (low, high) in enumerate(zip(bounds, bounds[1:]))
    ]
    for copy in copies:
        copy.start()
    return copies


def each(low, high, body):
    lax.fori_loop(low, high, lambda i, c: (body(i), c)[1], 0)


def borders(above, below, left, right, rim, pair, sems):
    rows, cols = left.shape[0], above.shape[1] - 8
    copies = [
        pltpu.make_async_copy(x, to, sems.at[n])
        for n, (x, to) in enumerate(
            (
                (left, pair.at[0, pl.ds(2, rows)]),
                (right, pair.at[1, pl.ds(2, rows)]),
                (above, rim.at[0]),
                (below, rim.at[1]),
            )
        )
    ]
    for copy in copies:
        copy.start()
    for copy in copies:
        copy.wait()
    for n in range(2):
        at = slice(cols + 2 * n, cols + 2 * n + 2)
        pair[n, 0:2] = rim[0, :, at]
        pair[n, rows + 2 :] = rim[1, :, at]


def shift_rows(low, high, begin, grad, pair, wide):
    cols, chans = grad.shape[1:]

    def put(i):
        row = grad[i]
        wide[i, :, :chans] = jnp.concatenate([row[2:], pair[1, begin + i]], axis=0)
        wide[i, :, chans : 2 * chans] = row
        wide[i, :, 2 * chans :] = jnp.concatenate(
            [pair[0, begin + i], row[: cols - 2]], axis=0
        )

    each(low, high, put)


def four_products(feat, wide, first, fold):
    cols, chans = feat.shape[1:]
    lanes = wide.shape[2]
    fs, ds = [[], [], [], []], [[], [], [], []]
    for u in range(fold):
        i = first + 4 * u
        f0 = feat[pl.ds(i, 2)].reshape(2 * cols, chans)
        f1 = feat[pl.ds(i + 2, 2)].reshape(2 * cols, chans)
        d = [wide[pl.ds(i + 2 * k, 2)].reshape(2 * cols, lanes) for k in range(4)]
        for n, v in enumerate((f0, f0 + f1, f0 - f1, f1)):
            fs[n].append(v)
        for n, v in enumerate((d[0] - d[2], d[1] + d[2], d[1] - d[2], d[3] - d[1])):
            ds[n].append(v)
    return [
        lax.dot_general(
            jnp.concatenate(f, axis=0),
            jnp.concatenate(d, axis=0),
            (((0,), (0,)), ((), ())),
            preferred_element_type=F32,
        )
        for f, d in zip(fs, ds)
    ]


def products(
    blocks, fold, feat_hbm, grad_hbm, above, below, left, right, out,
    feat, grad, wide, rim, pair, feat_sems, grad_sems, rim_sems,
):
    rows, cols, _ = feat.shape
    edges = [sum(blocks[:n]) for n in range(len(blocks) + 1)]
    grads = fetch(
        grad_hbm, grad, grad_sems, [0, *(e + 2 for e in edges[1:-1]), rows], 2
    )
    feats = fetch(feat_hbm, feat, feat_sems, edges, 0)
    borders(above, below, left, right, rim, pair, rim_sems)
    grad[0:2] = rim[0, :, :cols]
    grad[rows + 2 :] = rim[1, :, :cols]
    made = 0
    for t, first in enumerate(edges[:-1]):
        grads[t].wait()
        feats[t].wait()
        shift_rows(made, edges[t + 1] + 4, 0, grad, pair, wide)
        made = edges[t + 1] + 4
        for i in range(first, edges[t + 1], 4 * fold):
            for n, v in enumerate(four_products(feat, wide, i, fold)):
                if i == 0:
                    out[n] = v
                else:
                    out[n] += v


def columns(taps):
    rows = jnp.zeros((128 - taps.shape[0], taps.shape[1]), F32)
    return jnp.concatenate([taps[...].astype(F32), rows], axis=0).T


def finish(prods, point, taps, out, whole_point, stage, sem):
    chans = point.shape[0]
    x = point[...].astype(F32)
    p = jnp.concatenate([x[:, 0], x[:, 1]], axis=1)
    whole_point[...] = p.astype(BF16)
    w = columns(taps)
    acc = jnp.zeros((chans, chans), F32)
    lane = lax.broadcasted_iota(jnp.int32, (chans, 128), 1)
    sums = jnp.zeros((chans, 128), F32)
    for b in range(3):
        at = slice(b * chans, (b + 1) * chans)
        one, two, three, four = (prods[n, :, at] for n in range(4))
        half = 0.5 * (two - three)
        for a, m in enumerate((four + half, 0.5 * (two + three), one + half)):
            k = 3 * a + b
            acc = acc + w[:, k : k + 1] * m
            sums = jnp.where(lane == k, jnp.sum(p * m, axis=1, keepdims=True), sums)
    groups = out.shape[0]
    share = chans // groups
    tap_rows = sums.T[:16]
    for s in range(groups):
        stage[s, :share] = acc[s * share : (s + 1) * share]
        stage[s, share:] = tap_rows
    copy = pltpu.make_async_copy(stage, out, sem)
    copy.start()
    copy.wait()


def second(got, done, out):
    del done
    total = got[0]
    for s in range(1, got.shape[0]):
        total = total + got[s]
    rows = total.shape[0] // 2
    tap = total[rows:]
    sub = lax.broadcasted_iota(jnp.int32, tap.shape, 0)
    for r in range(out.shape[0]):
        out[r] = jnp.where(sub == 9, total[r : r + 1], tap)


def third(scale, got, taps, row):
    total = got[0]
    for s in range(1, got.shape[0]):
        total = total + got[s]
    total = total * scale
    taps[...] = total[:9]
    row[...] = total[9:10]


def rows_back(
    begin, count, step, grad_hbm, above, below, left, right, weights, out,
    grad, wide, rim, pair, stage, grad_sems, rim_sems, out_sem,
):
    rows, cols, chans = out.shape
    low, high = max(begin - 2, 0), min(begin + count + 2, rows)
    waits = fetch(grad_hbm, grad, grad_sems, [low, high], 2 - begin)
    borders(above, below, left, right, rim, pair, rim_sems)
    if begin == 0:
        grad[0:2] = rim[0, :, :cols]
    if begin + count == rows:
        grad[count + 2 :] = rim[1, :, :cols]
    for copy in waits:
        copy.wait()
    shift_rows(0, count + 4, begin, grad, pair, wide)
    for t in range(0, count, step):
        acc = None
        for a in range(3):
            lhs = wide[pl.ds(t + 4 - 2 * a, step)]
            term = lax.dot_general(
                lhs.reshape(step * cols, 3 * chans),
                weights[a],
                (((1,), (1,)), ((), ())),
                preferred_element_type=F32,
            )
            acc = term if acc is None else acc + term
        stage[pl.ds(t, step)] = acc.reshape(step, cols, chans).astype(BF16)
    copy = pltpu.make_async_copy(stage, out.at[pl.ds(begin, count)], out_sem)
    copy.start()
    copy.wait()


def back_one(
    count, step, grad_hbm, above, below, left, right, point, taps, out, weights, done, *scratch
):
    chans = point.shape[0]
    p = point[...].astype(F32)
    w = columns(taps)
    for k in range(9):
        weights[k // 3, :, (k % 3) * chans : (k % 3 + 1) * chans] = (
            p * w[:, k : k + 1]
        ).astype(BF16)
    rows_back(
        0, count, step, grad_hbm, above, below, left, right, weights, out, *scratch
    )
    done[...] = jnp.zeros_like(done)


def back_two(
    begin, count, step, grad_hbm, above, below, left, right, weights, half, out, *scratch
):
    del half
    rows_back(
        begin, count, step, grad_hbm, above, below, left, right, weights, out, *scratch
    )


def moved(x, axis, by):
    count = lax.axis_size(axis)
    pairs = [(i, i + by) for i in range(count) if 0 <= i + by < count]
    return lax.ppermute(x, axis, pairs)


def swapped(x, axes):
    return lax.all_to_all(x, axes, 0, 0, tiled=True)


def on_device(features, out_grad, depth_weight, point_weight):
    stay = pltpu.with_memory_space_constraint
    feat, grad = (stay(x[0], pltpu.HBM) for x in (features, out_grad))
    rows, cols, chans = feat.shape
    place, every = ("row", "col"), ("slide", "row", "col")
    slides, places = lax.axis_size("slide"), lax.axis_size(place)
    scale = 1.0 / math.sqrt(slides * places * rows * cols)
    macs = rows * cols * chans * chans
    shape = jax.ShapeDtypeStruct
    hbm = pl.BlockSpec(memory_space=pltpu.HBM)
    vmem, dma = pltpu.VMEM, pltpu.SemaphoreType.DMA

    mine, top, bottom, lo, hi = whole(
        prepare,
        [
            shape((slides * places, 2, chans // 2), BF16),
            *[shape((2, cols, chans), BF16)] * 2,
            *[shape((rows, 2, chans), BF16)] * 2,
        ],
        (point_weight, grad),
        "prepare",
        1 << 20,
        4,
        [*[vmem((rows, 8, chans), BF16)] * 2, dma((4,))],
        ([IN_VMEM, hbm], [IN_VMEM] * 5),
    )
    point = swapped(mine, every)
    left = moved(hi, "col", 1)
    right = moved(lo, "col", -1)
    top, bottom = whole(
        ends,
        [shape((2, cols + 8, chans), BF16)] * 2,
        (top, bottom, left, right),
        "ends",
        1 << 10,
        2,
    )
    above = moved(bottom, "row", 1)
    below = moved(top, "row", -1)
    halo = (grad, *(stay(x, pltpu.HBM) for x in (above, below, left, right)))
    halo_specs = [hbm] * 5

    def buffers(count):
        return [
            vmem((count + 4, cols, chans), BF16),
            vmem((count + 4, cols, 3 * chans), BF16),
            vmem((2, 2, cols + 8, chans), BF16),
            vmem((2, rows + 4, 2, chans), BF16),
        ]

    blocks = (16, rows - 16)
    (prods,) = whole(
        functools.partial(products, blocks, 4),
        [shape((4, chans, 3 * chans), F32)],
        (feat, *halo),
        "products",
        12 * macs,
        46,
        [
            vmem((rows, cols, chans), BF16),
            *buffers(rows),
            *[dma((len(blocks),))] * 2,
            dma((4,)),
        ],
        ([hbm, *halo_specs], [IN_VMEM]),
    )
    parts, point = whole(
        finish,
        [pltpu.HBM((slides, 32, chans), F32), shape((chans, chans), BF16)],
        (prods, point, depth_weight),
        "finish",
        36 * chans * chans,
        8,
        [vmem((slides, 32, chans), F32), dma],
        ([IN_VMEM] * 3, [hbm, IN_VMEM]),
    )
    got = swapped(parts, "slide")

    early, step = 40, 8

    def scratch(count):
        return [
            *buffers(count),
            vmem((count, cols, chans), BF16),
            dma((1,)),
            dma((4,)),
            dma,
        ]

    half, weights, done = whole(
        functools.partial(back_one, early, step),
        [
            shape((rows, cols, chans), BF16),
            shape((3, chans, 3 * chans), BF16),
            shape((8, 128), F32),
        ],
        (*halo, point, depth_weight),
        "back_one",
        18 * macs * early // rows,
        40,
        scratch(early),
        ([*halo_specs, IN_VMEM, IN_VMEM], [hbm, IN_VMEM, IN_VMEM]),
    )
    (parts,) = whole(
        second, [shape((places, 16, chans), F32)], (got, done), "second", 1 << 20, 4
    )
    got = swapped(parts, place)
    (feature_grad,) = whole(
        functools.partial(back_two, early, rows - early, step),
        [shape((rows, cols, chans), BF16)],
        (*halo, weights, stay(half, pltpu.HBM)),
        "back_two",
        18 * macs * (rows - early) // rows,
        32,
        scratch(rows - early),
        ([*halo_specs, IN_VMEM, hbm], [hbm]),
        {6: 0},
    )
    depth_grad, point_grad = whole(
        functools.partial(third, scale),
        [shape((9, chans), F32), shape((1, chans), F32)],
        (got,),
        "third",
        1 << 20,
        4,
    )
    return feature_grad[None], point_grad, depth_grad


def solution(mesh):
    placed = (
        P("slide", "row", "col", None),
        P("slide", "row", "col", None),
        P(),
        P(("slide", "row", "col"), None),
    )
    return jax.shard_map(
        on_device,
        mesh=mesh,
        in_specs=placed,
        out_specs=(P("slide", "row", "col", None), P(("slide", "row", "col"), None), P()),
        check_vma=False,
    )
```

time: 111 us -> 90.5 us (0.82)
  blocking collectives: 16.6 us -> 0 us
  starting transfers between devices: 39.4 us -> 46.3 us
  local copies, waits for them, and re-layouts: 7.11 us -> 1.37 us
  Pallas kernels: 37.7 us -> 34.9 us
  other arithmetic: 1.6 us -> 0 us
    all_to_all x1 -> x0, blocking collectives: 16.6 us -> none  [on_device(): got = lax.all_to_all(parts, 'slide', 0, 0, tiled=True)]
    all_to_all x3, starting transfers between devices: 23.5 us -> 29 us  [swapped(): return lax.all_to_all(x, axes, 0, 0, tiled=True)]
    all_to_all x3, waiting for transfers between devices: 6.09 us -> 2.66 us  [swapped(): return lax.all_to_all(x, axes, 0, 0, tiled=True)]
    ppermute x4, waiting for transfers between devices: 0.93 us -> 3.89 us  [moved(): return lax.ppermute(x, axis, pairs)]
    pallas_call x5 -> x8, Pallas kernels: 37.7 us -> 34.9 us  [whole(): pl.pallas_call(body, out_shape=outs, in_specs=ins, out_specs=outs_at, scr...]
    slice x4 -> x0, local copies, waits for them, and re-layouts: 2.14 us -> none  [the longest x3 1.16 us: on_device(): x[:, s]]
    unnamed x17 -> x12, local copies, waits for them, and re-layouts: 2.96 us -> 1.37 us
    ppermute x4, starting transfers between devices: 15.9 us -> 17.3 us  [moved(): return lax.ppermute(x, axis, pairs)]
  transfers between devices with their start and end apart: 7 -> 7, of which waited for: 2 -> 4; matrix products, arithmetic and copies ran while one was open for 5% -> 0% of each run, Pallas kernels for 32% -> 33%
where the time goes in v2:
time: 90.5 us; the launch traced here: 89.9 us
  starting transfers between devices  46.3 us (51%)
  Pallas kernels  34.9 us (39%)
  waiting for transfers between devices  6.55 us (7%)
  local copies, waits for them, and re-layouts  1.37 us (2%)
    pallas_call x8, Pallas kernels, whole(): pl.pallas_call(body, out_shape=outs, in_specs=ins, out_specs=outs_at, scr...  34.9 us
    all_to_all x3, starting transfers between devices, swapped(): return lax.all_to_all(x, axes, 0, 0, tiled=True)  29 us
    ppermute x4, starting transfers between devices, moved(): return lax.ppermute(x, axis, pairs)  17.3 us
    ppermute x4, waiting for transfers between devices, moved(): return lax.ppermute(x, axis, pairs)  3.89 us
    all_to_all x3, waiting for transfers between devices, swapped(): return lax.all_to_all(x, axes, 0, 0, tiled=True)  2.66 us
  transfers between devices with their start and end apart: 7, of which 4 were waited for; matrix products, arithmetic and copies ran while one was open for 0% of the time, Pallas kernels for 33%

profile of v2, /device:TPU:1, one launch (start us, length us, event | category | flops | bytes accessed | tf_op | source)
XLA Modules:
  0.0 89.9 jit_solution(6961186740383684916)
XLA Ops:
  0.6 0.0 copy-start.3
  0.6 0.7 copy-done.3
  1.3 1.8 %prepare.1 = (bf16[256,2,128]{2,1,0:T(2,128)(2,1)}, bf16[2,128,256]{2,1,0:T(8,128)(2,1)S(1)}, bf16[2,128,256]{2,1,0:T(8,128)(2,1)S(1)}, bf16[64,2,256]{2,1,0:T(2,128)(2,1)S(1)}, bf16[64,2,256]{2,1,0:T(2,128)(2,1)S(1)}) custom-call(bf16[1,256]{1,0:T(2,128)(2,1)S(1)} %copy-done.3, bf16[64,128,256]{2,1,0:T(8,128)(2,1)} %bitcast.3), custom_call_target="tpu_custom_call" | custom-call | flops 1048576 | bytes 4719104 | tf_op jit(solution)/shard_map/prepare/pallas_call | solution.py:19
  3.1 4.4 %collective-permute-start = (bf16[64,2,256]{2,1,0:T(2,128)(2,1)S(1)}, bf16[64,2,256]{2,1,0:T(2,128)(2,1)S(1)}, u32[]{:S(2)}, u32[]{:S(2)}) collective-permute-start(bf16[64,2,256]{2,1,0:T(2,128)(2,1)S(1)} %get-tuple-element.19), channel_id=1, source_target_pairs={{0,1},{1,2},{2,3},{4,5},{5,6},{6,7},{8,9},{9,10},{10,11},{12,13},{... | collective-permute-start | bytes 196616 | tf_op jit(solution)/shard_map/ppermute | solution.py:290
  7.5 1.3 %collective-permute-start.1 = (bf16[64,2,256]{2,1,0:T(2,128)(2,1)S(1)}, bf16[64,2,256]{2,1,0:T(2,128)(2,1)S(1)}, u32[]{:S(2)}, u32[]{:S(2)}) collective-permute-start(bf16[64,2,256]{2,1,0:T(2,128)(2,1)S(1)} %get-tuple-element.20), channel_id=1, source_target_pairs={{1,0},{2,1},{3,2},{5,4},{6,5},{7,6},{9,8},{10,9},{11,10},{13,12},{... | collective-permute-start | bytes 196616 | tf_op jit(solution)/shard_map/ppermute | solution.py:290
  8.8 0.0 collective-permute-done.left
  8.8 0.0 copy-start
  8.8 3.9 %collective-permute-done.1.right = bf16[64,2,256]{2,1,0:T(2,128)(2,1)S(1)} collective-permute-done((bf16[64,2,256]{2,1,0:T(2,128)(2,1)S(1)}, bf16[64,2,256]{2,1,0:T(2,128)(2,1)S(1)}, u32[]{:S(2)}, u32[]{:S(2)}) %collective-permute-start.1) | collective-permute-done | bytes 65568 | tf_op jit(solution)/shard_map/ppermute | solution.py:290
  12.7 0.0 copy-start.1
  12.7 9.7 %collective-permute-start.2 = (bf16[2,136,256]{2,1,0:T(8,128)(2,1)S(1)}, bf16[2,136,256]{2,1,0:T(8,128)(2,1)S(1)}, u32[]{:S(2)}, u32[]{:S(2)}) collective-permute-start(bf16[2,136,256]{2,1,0:T(8,128)(2,1)S(1)} %get-tuple-element.21), channel_id=1, source_target_pairs={{0,4},{4,8},{8,12},{1,5},{5,9},{9,13},{2,6},{6,10},{10,14},{3,7},{... | collective-permute-start | bytes 417800 | tf_op jit(solution)/shard_map/ppermute | solution.py:290
  22.5 1.9 %collective-permute-start.3 = (bf16[2,136,256]{2,1,0:T(8,128)(2,1)S(1)}, bf16[2,136,256]{2,1,0:T(8,128)(2,1)S(1)}, u32[]{:S(2)}, u32[]{:S(2)}) collective-permute-start(bf16[2,136,256]{2,1,0:T(8,128)(2,1)S(1)} %get-tuple-element.22), channel_id=1, source_target_pairs={{4,0},{8,4},{12,8},{5,1},{9,5},{13,9},{6,2},{10,6},{14,10},{7,3},{... | collective-permute-start | bytes 417800 | tf_op jit(solution)/shard_map/ppermute | solution.py:290
  24.4 13.0 %all-to-all-start = ((bf16[256,2,128]{2,1,0:T(2,128)(2,1)}), bf16[256,2,128]{2,1,0:T(2,128)(2,1)S(1)}, u32[]{:S(2)}, u32[]{:S(2)}) async-start(bf16[256,2,128]{2,1,0:T(2,128)(2,1)} %get-tuple-element.23), calls=%async_computation | async-start | bytes 262144 | tf_op jit(solution)/shard_map/all_to_all | solution.py:294
  37.4 0.0 collective-permute-done.2.above
  37.4 0.0 copy-start.4
  37.4 0.0 collective-permute-done.3.below
  37.4 0.0 copy-start.5
  37.4 0.7 copy-done.5
  38.1 0.0 copy-done
  38.1 0.0 copy-done.1
  38.1 0.0 copy-done.4
  38.1 0.0 copy-start.2
  38.1 11.8 %products.1.prods = f32[4,256,768]{2,1,0:T(8,128)S(1)} custom-call(bf16[64,128,256]{2,1,0:T(8,128)(2,1)} %bitcast.8, bf16[64,128,256]{2,1,0:T(8,128)(2,1)} %bitcast.4, bf16[2,136,256]{2,1,0:T(8,128)(2,1)} %copy-done.4, bf16[2,136,256]{2,1,0:T(8,128)(2,1)} %copy-done.5, bf16[64,2,256]{2,1,0:T(2,128)(2,1)} %copy-done, bf16[64,2,256]{2,1,0:T(2,128)(2,1)} %copy-done.1), custom_call_target="tpu_custom_call" | custom-call | flops 6442450944 | bytes 11943936 | tf_op jit(solution)/shard_map/products/pallas_call | solution.py:19
  50.0 0.3 all-to-all-done.point
  50.2 0.0 copy-done.2
  50.2 2.0 %finish.1 = (f32[16,32,256]{2,1,0:T(8,128)}, bf16[256,256]{1,0:T(8,128)(2,1)S(1)}) custom-call(f32[4,256,768]{2,1,0:T(8,128)S(1)} %products.1.prods, bf16[256,2,128]{2,1,0:T(2,128)(2,1)S(1)} %all-to-all-done.point, bf16[9,256]{1,0:T(8,128)(2,1)S(1)} %copy-done.2), custom_call_target="tpu_custom_call" | custom-call | flops 2359296 | bytes 3936768 | tf_op jit(solution)/shard_map/finish/pallas_call | solution.py:19
  52.2 6.5 %all-to-all-start.1 = ((f32[16,32,256]{2,1,0:T(8,128)}), f32[16,32,256]{2,1,0:T(8,128)S(1)}, u32[]{:S(2)}, u32[]{:S(2)}) async-start(f32[16,32,256]{2,1,0:T(8,128)} %get-tuple-element.27), calls=%async_computation.1 | async-start | bytes 1048576 | tf_op jit(solution)/shard_map/all_to_all | solution.py:294
  58.7 10.7 %back_one.1 = (bf16[64,128,256]{2,1,0:T(8,128)(2,1)}, bf16[3,256,768]{2,1,0:T(8,128)(2,1)S(1)}, f32[8,128]{1,0:T(8,128)S(1)}) custom-call(bf16[64,128,256]{2,1,0:T(8,128)(2,1)} %bitcast.5, bf16[2,136,256]{2,1,0:T(8,128)(2,1)} %copy-done.4, bf16[2,136,256]{2,1,0:T(8,128)(2,1)} %copy-done.5, bf16[64,2,256]{2,1,0:T(2,128)(2,1)} %copy-done, ...), custom_call_target="tpu_custom_call" | custom-call | flops 6039797760 | bytes 10117632 | tf_op jit(solution)/shard_map/back_one/pallas_call | solution.py:19
  69.4 0.1 all-to-all-done.1.got
  69.4 0.7 second.1
  70.2 9.5 %all-to-all-start.2 = ((f32[16,16,256]{2,1,0:T(8,128)}), f32[16,16,256]{2,1,0:T(8,128)S(1)}, u32[]{:S(2)}, u32[]{:S(2)}) async-start(f32[16,16,256]{2,1,0:T(8,128)} %second.1), calls=%async_computation.2 | async-start | bytes 524288 | tf_op jit(solution)/shard_map/all_to_all | solution.py:294
  79.7 7.2 %back_two.1 = bf16[64,128,256]{2,1,0:T(8,128)(2,1)} custom-call(bf16[64,128,256]{2,1,0:T(8,128)(2,1)} %bitcast.6, bf16[2,136,256]{2,1,0:T(8,128)(2,1)} %copy-done.4, bf16[2,136,256]{2,1,0:T(8,128)(2,1)} %copy-done.5, bf16[64,2,256]{2,1,0:T(2,128)(2,1)} %copy-done, bf16[64,2,256]{2,1,0:T(2,128)(2,1)} %copy-done.1, ...), custom_call_target="tpu_custom_call", output_to_operand_aliasing={{}: (6, {})} | custom-call | flops 3623878656 | bytes 14172160 | tf_op jit(solution)/shard_map/back_two/pallas_call | solution.py:19
  86.9 2.3 %all-to-all-done.2.got = f32[16,16,256]{2,1,0:T(8,128)S(1)} async-done(((f32[16,16,256]{2,1,0:T(8,128)}), f32[16,16,256]{2,1,0:T(8,128)S(1)}, u32[]{:S(2)}, u32[]{:S(2)}) %all-to-all-start.2) | async-done | bytes 262176 | tf_op jit(solution)/shard_map/all_to_all | solution.py:294
  89.2 0.6 third.1
  (1 shorter events, 0.0 us)
Async XLA Ops:
  0.6 0.7 copy-start.3
  3.1 5.7 %collective-permute-start = (bf16[64,2,256]{2,1,0:T(2,128)(2,1)S(1)}, bf16[64,2,256]{2,1,0:T(2,128)(2,1)S(1)}, u32[]{:S(2)}, u32[]{:S(2)}) collective-permute-start(bf16[64,2,256]{2,1,0:T(2,128)(2,1)S(1)} %get-tuple-element.19), channel_id=1, source_target_pairs={{0,1},{1,2},{2,3},{4,5},{5,6},{6,7},{8,9},{9,10},{10,11},{12,13},{... | collective-permute-start | bytes 196616 | tf_op jit(solution)/shard_map/ppermute | solution.py:290
  7.5 5.2 %collective-permute-start.1 = (bf16[64,2,256]{2,1,0:T(2,128)(2,1)S(1)}, bf16[64,2,256]{2,1,0:T(2,128)(2,1)S(1)}, u32[]{:S(2)}, u32[]{:S(2)}) collective-permute-start(bf16[64,2,256]{2,1,0:T(2,128)(2,1)S(1)} %get-tuple-element.20), channel_id=1, source_target_pairs={{1,0},{2,1},{3,2},{5,4},{6,5},{7,6},{9,8},{10,9},{11,10},{13,12},{... | collective-permute-start | bytes 196616 | tf_op jit(solution)/shard_map/ppermute | solution.py:290
  8.8 29.3 %copy-start = (bf16[64,2,256]{2,1,0:T(2,128)(2,1)}, bf16[64,2,256]{2,1,0:T(2,128)(2,1)S(1)}, u32[]{:S(2)}) copy-start(bf16[64,2,256]{2,1,0:T(2,128)(2,1)S(1)} %collective-permute-done.left) | copy-start | bytes 196612
  12.7 25.4 %copy-start.1 = (bf16[64,2,256]{2,1,0:T(2,128)(2,1)}, bf16[64,2,256]{2,1,0:T(2,128)(2,1)S(1)}, u32[]{:S(2)}) copy-start(bf16[64,2,256]{2,1,0:T(2,128)(2,1)S(1)} %collective-permute-done.1.right) | copy-start | bytes 196612
  12.7 24.7 %collective-permute-start.2 = (bf16[2,136,256]{2,1,0:T(8,128)(2,1)S(1)}, bf16[2,136,256]{2,1,0:T(8,128)(2,1)S(1)}, u32[]{:S(2)}, u32[]{:S(2)}) collective-permute-start(bf16[2,136,256]{2,1,0:T(8,128)(2,1)S(1)} %get-tuple-element.21), channel_id=1, source_target_pairs={{0,4},{4,8},{8,12},{1,5},{5,9},{9,13},{2,6},{6,10},{10,14},{3,7},{... | collective-permute-start | bytes 417800 | tf_op jit(solution)/shard_map/ppermute | solution.py:290
  22.5 15.0 %collective-permute-start.3 = (bf16[2,136,256]{2,1,0:T(8,128)(2,1)S(1)}, bf16[2,136,256]{2,1,0:T(8,128)(2,1)S(1)}, u32[]{:S(2)}, u32[]{:S(2)}) collective-permute-start(bf16[2,136,256]{2,1,0:T(8,128)(2,1)S(1)} %get-tuple-element.22), channel_id=1, source_target_pairs={{4,0},{8,4},{12,8},{5,1},{9,5},{13,9},{6,2},{10,6},{14,10},{7,3},{... | collective-permute-start | bytes 417800 | tf_op jit(solution)/shard_map/ppermute | solution.py:290
  24.4 25.8 %all-to-all-start = ((bf16[256,2,128]{2,1,0:T(2,128)(2,1)}), bf16[256,2,128]{2,1,0:T(2,128)(2,1)S(1)}, u32[]{:S(2)}, u32[]{:S(2)}) async-start(bf16[256,2,128]{2,1,0:T(2,128)(2,1)} %get-tuple-element.23), calls=%async_computation | async-start | bytes 262144 | tf_op jit(solution)/shard_map/all_to_all | solution.py:294
  37.4 0.7 copy-start.4
  37.4 0.7 copy-start.5
  38.1 12.1 %copy-start.2 = (bf16[9,256]{1,0:T(8,128)(2,1)S(1)}, bf16[9,256]{1,0:T(8,128)(2,1)}, u32[]{:S(2)}) copy-start(bf16[9,256]{1,0:T(8,128)(2,1)} %taps.3) | copy-start | bytes 13828
  52.2 17.2 %all-to-all-start.1 = ((f32[16,32,256]{2,1,0:T(8,128)}), f32[16,32,256]{2,1,0:T(8,128)S(1)}, u32[]{:S(2)}, u32[]{:S(2)}) async-start(f32[16,32,256]{2,1,0:T(8,128)} %get-tuple-element.27), calls=%async_computation.1 | async-start | bytes 1048576 | tf_op jit(solution)/shard_map/all_to_all | solution.py:294
  70.2 19.1 %all-to-all-start.2 = ((f32[16,16,256]{2,1,0:T(8,128)}), f32[16,16,256]{2,1,0:T(8,128)S(1)}, u32[]{:S(2)}, u32[]{:S(2)}) async-start(f32[16,16,256]{2,1,0:T(8,128)} %second.1), calls=%async_computation.2 | async-start | bytes 524288 | tf_op jit(solution)/shard_map/all_to_all | solution.py:294

commit v3 on v2

--- a/solution.py
+++ b/solution.py
@@ -31,7 +31,11 @@
     )(*args)
 
 
-def prepare(row, grad, rows_out, top, bottom, lo, hi, first, last, sems):
+def either(flag, x, y):
+    return jnp.where(flag, x, y), jnp.where(flag, y, x)
+
+
+def prepare(weight, taps, grad, top, bottom, near, far, taps_out, first, last, row, sems):
     rows, cols, _ = grad.shape
     copies = [
         pltpu.make_async_copy(a, b, sems.at[n])
@@ -39,6 +43,8 @@
             (
                 (grad.at[:, pl.ds(0, 8)], first),
                 (grad.at[:, pl.ds(cols - 8, 8)], last),
+                (weight, row),
+                (taps, taps_out),
                 (grad.at[pl.ds(0, 2)], top),
                 (grad.at[pl.ds(rows - 2, 2)], bottom),
             )
@@ -46,25 +52,42 @@
     ]
     for copy in copies:
         copy.start()
-    half = row.shape[1] // 2
-    r = row[...].astype(F32)
-    two = jnp.concatenate([r[:, :half], r[:, half:]], axis=0).astype(BF16)
-    rows_out[...] = jnp.broadcast_to(two[None], rows_out.shape)
     for copy in copies:
         copy.wait()
-    lo[...] = first[:, :2]
-    hi[...] = last[:, 6:]
-
-
-def ends(top, bottom, left, right, top_out, bottom_out):
-    rows = left.shape[0]
+    even = lax.axis_index("pair") == 0
+    near[:rows], far[:rows] = either(even, last[:, 6:], first[:, :2])
+    twice = jnp.broadcast_to(row[...].astype(F32), (2, row.shape[1])).astype(BF16)
+    near[rows] = twice
+    far[rows] = twice
+
+
+def ends(
+    mine, top, bottom, near, far, two_rows, near_out, far_out, left_out, right_out, side, sems
+):
+    rows = near.shape[0] - 1
     cols = top.shape[1]
-    for out, part, at in ((top_out, top, 0), (bottom_out, bottom, rows - 2)):
-        out[:, :cols] = part[...]
-        fill = jnp.zeros((2, 4, left.shape[2]), BF16)
-        out[:, cols:] = jnp.concatenate(
-            [left[at : at + 2], right[at : at + 2], fill], axis=1
-        )
+    even = lax.axis_index("pair") == 0
+    low, high = either(even, mine[rows].astype(F32), near[rows].astype(F32))
+    pair = jnp.concatenate([low[:1], high[:1]], axis=0).astype(BF16)
+    two_rows[...] = jnp.broadcast_to(pair[None], two_rows.shape)
+    right, left = either(even, near[:rows], far[:rows])
+    side[0], side[1] = left, right
+    copies = [
+        pltpu.make_async_copy(side.at[n], to, sems.at[n])
+        for n, to in enumerate((left_out, right_out))
+    ]
+    for copy in copies:
+        copy.start()
+    fill = jnp.zeros((2, 4, near.shape[2]), BF16)
+    upper, lower = (
+        jnp.concatenate([left[at : at + 2], right[at : at + 2], fill], axis=1)
+        for at in (0, rows - 2)
+    )
+    even = lax.rem(lax.axis_index("row"), 2) == 0
+    near_out[:, :cols], far_out[:, :cols] = either(even, bottom[...], top[...])
+    near_out[:, cols:], far_out[:, cols:] = either(even, lower, upper)
+    for copy in copies:
+        copy.wait()
 
 
 def fetch(source, target, sems, bounds, offset):
@@ -83,29 +106,6 @@
 
 def each(low, high, body):
     lax.fori_loop(low, high, lambda i, c: (body(i), c)[1], 0)
-
-
-def borders(above, below, left, right, rim, pair, sems):
-    rows, cols = left.shape[0], above.shape[1] - 8
-    copies = [
-        pltpu.make_async_copy(x, to, sems.at[n])
-        for n, (x, to) in enumerate(
-            (
-                (left, pair.at[0, pl.ds(2, rows)]),
-                (right, pair.at[1, pl.ds(2, rows)]),
-                (above, rim.at[0]),
-                (below, rim.at[1]),
-            )
-        )
-    ]
-    for copy in copies:
-        copy.start()
-    for copy in copies:
-        copy.wait()
-    for n in range(2):
-        at = slice(cols + 2 * n, cols + 2 * n + 2)
-        pair[n, 0:2] = rim[0, :, at]
-        pair[n, rows + 2 :] = rim[1, :, at]
 
 
 def shift_rows(low, high, begin, grad, pair, wide):
@@ -147,18 +147,48 @@
 
 
 def products(
-    blocks, fold, feat_hbm, grad_hbm, above, below, left, right, out,
-    feat, grad, wide, rim, pair, feat_sems, grad_sems, rim_sems,
+    blocks, fold, feat_hbm, grad_hbm, near_hbm, far_hbm, left, right,
+    out, rim_out, pair_out, feat, grad, wide, pair, got, feat_sems, grad_sems, sems,
 ):
     rows, cols, _ = feat.shape
     edges = [sum(blocks[:n]) for n in range(len(blocks) + 1)]
+    waits = [
+        pltpu.make_async_copy(x, to, sems.at[3 + n])
+        for n, (x, to) in enumerate(
+            (
+                (left, pair.at[0, pl.ds(2, rows)]),
+                (right, pair.at[1, pl.ds(2, rows)]),
+                (near_hbm, got.at[0]),
+                (far_hbm, got.at[1]),
+            )
+        )
+    ]
+    for copy in waits:
+        copy.start()
     grads = fetch(
         grad_hbm, grad, grad_sems, [0, *(e + 2 for e in edges[1:-1]), rows], 2
     )
     feats = fetch(feat_hbm, feat, feat_sems, edges, 0)
-    borders(above, below, left, right, rim, pair, rim_sems)
-    grad[0:2] = rim[0, :, :cols]
-    grad[rows + 2 :] = rim[1, :, :cols]
+    for copy in waits:
+        copy.wait()
+    even = lax.rem(lax.axis_index("row"), 2) == 0
+    below, above = either(even, got[0], got[1])
+    for at, part in ((0, above), (rows + 2, below)):
+        grad[at : at + 2] = part[:, :cols]
+        for n in range(2):
+            pair[n, at : at + 2] = part[:, cols + 2 * n : cols + 2 * n + 2]
+    copies = [
+        pltpu.make_async_copy(x, to, sems.at[n])
+        for n, (x, to) in enumerate(
+            (
+                (grad.at[pl.ds(0, 2)], rim_out.at[0]),
+                (grad.at[pl.ds(rows + 2, 2)], rim_out.at[1]),
+                (pair, pair_out),
+            )
+        )
+    ]
+    for copy in copies:
+        copy.start()
     made = 0
     for t, first in enumerate(edges[:-1]):
         grads[t].wait()
@@ -171,6 +201,8 @@
                     out[n] = v
                 else:
                     out[n] += v
+    for copy in copies:
+        copy.wait()
 
 
 def columns(taps):
@@ -178,10 +210,15 @@
     return jnp.concatenate([taps[...].astype(F32), rows], axis=0).T
 
 
-def finish(prods, point, taps, out, whole_point, stage, sem):
-    chans = point.shape[0]
+def finish(prods, point, taps, out, whole_point, stage, natural, sem):
+    chans = taps.shape[1]
     x = point[...].astype(F32)
-    p = jnp.concatenate([x[:, 0], x[:, 1]], axis=1)
+    lanes = natural.shape[2]
+    for n in range(2):
+        for h in range(2):
+            part = x[:, n, h * lanes : (h + 1) * lanes]
+            natural[h, pl.ds(n, chans // 2, stride=2)] = part
+    p = jnp.concatenate([natural[0], natural[1]], axis=1)
     whole_point[...] = p.astype(BF16)
     w = columns(taps)
     acc = jnp.zeros((chans, chans), F32)
@@ -228,17 +265,28 @@
 
 
 def rows_back(
-    begin, count, step, grad_hbm, above, below, left, right, weights, out,
-    grad, wide, rim, pair, stage, grad_sems, rim_sems, out_sem,
+    begin, count, step, grad_hbm, rim, pair_hbm, weights, out,
+    grad, wide, pair, stage, sems,
 ):
     rows, cols, chans = out.shape
     low, high = max(begin - 2, 0), min(begin + count + 2, rows)
-    waits = fetch(grad_hbm, grad, grad_sems, [low, high], 2 - begin)
-    borders(above, below, left, right, rim, pair, rim_sems)
+    parts = [(pair_hbm, pair)]
     if begin == 0:
-        grad[0:2] = rim[0, :, :cols]
+        parts.append((rim.at[0], grad.at[pl.ds(0, 2)]))
     if begin + count == rows:
-        grad[count + 2 :] = rim[1, :, :cols]
+        parts.append((rim.at[1], grad.at[pl.ds(count + 2, 2)]))
+    parts.append(
+        (
+            grad_hbm.at[pl.ds(low, high - low)],
+            grad.at[pl.ds(low - begin + 2, high - low)],
+        )
+    )
+    waits = [
+        pltpu.make_async_copy(x, to, sems.at[n]) for n, (x, to) in enumerate(parts)
+    ]
+    for copy in waits:
+        copy.start()
+    weights = weights()
     for copy in waits:
         copy.wait()
     shift_rows(0, count + 4, begin, grad, pair, wide)
@@ -254,40 +302,43 @@
             )
             acc = term if acc is None else acc + term
         stage[pl.ds(t, step)] = acc.reshape(step, cols, chans).astype(BF16)
-    copy = pltpu.make_async_copy(stage, out.at[pl.ds(begin, count)], out_sem)
+    copy = pltpu.make_async_copy(stage, out.at[pl.ds(begin, count)], sems.at[4])
     copy.start()
     copy.wait()
 
 
 def back_one(
-    count, step, grad_hbm, above, below, left, right, point, taps, out, weights, done, *scratch
+    count, step, grad_hbm, rim, pair_hbm, point, taps, out, weights, done, *scratch
 ):
     chans = point.shape[0]
-    p = point[...].astype(F32)
-    w = columns(taps)
-    for k in range(9):
-        weights[k // 3, :, (k % 3) * chans : (k % 3 + 1) * chans] = (
-            p * w[:, k : k + 1]
-        ).astype(BF16)
-    rows_back(
-        0, count, step, grad_hbm, above, below, left, right, weights, out, *scratch
-    )
+
+    def scaled():
+        p = point[...].astype(F32)
+        w = columns(taps)
+        for k in range(9):
+            weights[k // 3, :, (k % 3) * chans : (k % 3 + 1) * chans] = (
+                p * w[:, k : k + 1]
+            ).astype(BF16)
+        return weights
+
+    rows_back(0, count, step, grad_hbm, rim, pair_hbm, scaled, out, *scratch)
     done[...] = jnp.zeros_like(done)
 
 
 def back_two(
-    begin, count, step, grad_hbm, above, below, left, right, weights, half, out, *scratch
+    begin, count, step, grad_hbm, rim, pair_hbm, weights, half, out, *scratch
 ):
     del half
     rows_back(
-        begin, count, step, grad_hbm, above, below, left, right, weights, out, *scratch
-    )
-
-
-def moved(x, axis, by):
+        begin, count, step, grad_hbm, rim, pair_hbm, lambda: weights, out, *scratch
+    )
+
+
+def across(near, far, axis):
     count = lax.axis_size(axis)
-    pairs = [(i, i + by) for i in range(count) if 0 <= i + by < count]
-    return lax.ppermute(x, axis, pairs)
+    pairs = [(i, i ^ 1) for i in range(count)]
+    others = [(i, i + 1 if i % 2 else i - 1) for i in range(1, count - 1)]
+    return lax.ppermute(near, axis, pairs), lax.ppermute(far, axis, others)
 
 
 def swapped(x, axes):
@@ -298,7 +349,8 @@
     stay = pltpu.with_memory_space_constraint
     feat, grad = (stay(x[0], pltpu.HBM) for x in (features, out_grad))
     rows, cols, chans = feat.shape
-    place, every = ("row", "col"), ("slide", "row", "col")
+    col = ("half", "pair")
+    place = ("row", *col)
     slides, places = lax.axis_size("slide"), lax.axis_size(place)
     scale = 1.0 / math.sqrt(slides * places * rows * cols)
     macs = rows * cols * chans * chans
@@ -306,81 +358,85 @@
     hbm = pl.BlockSpec(memory_space=pltpu.HBM)
     vmem, dma = pltpu.VMEM, pltpu.SemaphoreType.DMA
 
-    mine, top, bottom, lo, hi = whole(
+    edge = shape((2, cols, chans), BF16)
+    side = shape((rows + 1, 2, chans), BF16)
+    top, bottom, near, far, taps = whole(
         prepare,
-        [
-            shape((slides * places, 2, chans // 2), BF16),
-            *[shape((2, cols, chans), BF16)] * 2,
-            *[shape((rows, 2, chans), BF16)] * 2,
-        ],
-        (point_weight, grad),
+        [edge, edge, side, side, shape((9, chans), BF16)],
+        (stay(point_weight, pltpu.HBM), stay(depth_weight, pltpu.HBM), grad),
         "prepare",
         1 << 20,
         4,
-        [*[vmem((rows, 8, chans), BF16)] * 2, dma((4,))],
-        ([IN_VMEM, hbm], [IN_VMEM] * 5),
-    )
-    point = swapped(mine, every)
-    left = moved(hi, "col", 1)
-    right = moved(lo, "col", -1)
-    top, bottom = whole(
+        [*[vmem((rows, 8, chans), BF16)] * 2, vmem((1, chans), BF16), dma((6,))],
+        ([hbm] * 3, [IN_VMEM] * 5),
+    )
+    edge = shape((2, cols + 8, chans), BF16)
+    two_rows, *edges, left, right = whole(
         ends,
-        [shape((2, cols + 8, chans), BF16)] * 2,
-        (top, bottom, left, right),
+        [
+            shape((slides * places // 2, 2, chans), BF16),
+            *[edge] * 2,
+            *[pltpu.HBM((rows, 2, chans), BF16)] * 2,
+        ],
+        (near, top, bottom, *across(near, far, col)),
         "ends",
         1 << 10,
-        2,
-    )
-    above = moved(bottom, "row", 1)
-    below = moved(top, "row", -1)
-    halo = (grad, *(stay(x, pltpu.HBM) for x in (above, below, left, right)))
-    halo_specs = [hbm] * 5
+        3,
+        [vmem((2, rows, 2, chans), BF16), dma((2,))],
+        ([IN_VMEM] * 5, [IN_VMEM] * 3 + [hbm] * 2),
+    )
+    rims = across(*edges, "row")
+    point = swapped(two_rows, ("slide", "row", "half"))
 
     def buffers(count):
         return [
             vmem((count + 4, cols, chans), BF16),
             vmem((count + 4, cols, 3 * chans), BF16),
-            vmem((2, 2, cols + 8, chans), BF16),
             vmem((2, rows + 4, 2, chans), BF16),
         ]
 
     blocks = (16, rows - 16)
-    (prods,) = whole(
+    prods, rim, pair = whole(
         functools.partial(products, blocks, 4),
-        [shape((4, chans, 3 * chans), F32)],
-        (feat, *halo),
+        [
+            shape((4, chans, 3 * chans), F32),
+            pltpu.HBM((2, 2, cols, chans), BF16),
+            pltpu.HBM((2, rows + 4, 2, chans), BF16),
+        ],
+        (feat, grad, *(stay(x, pltpu.HBM) for x in (*rims, left, right))),
         "products",
         12 * macs,
         46,
         [
             vmem((rows, cols, chans), BF16),
             *buffers(rows),
+            vmem((2, 2, cols + 8, chans), BF16),
             *[dma((len(blocks),))] * 2,
-            dma((4,)),
+            dma((7,)),
         ],
-        ([hbm, *halo_specs], [IN_VMEM]),
-    )
+        ([hbm] * 6, [IN_VMEM, hbm, hbm]),
+    )
+    halo = [grad, *(stay(x, pltpu.HBM) for x in (rim, pair))]
+    halo_specs = [hbm] * 3
     parts, point = whole(
         finish,
         [pltpu.HBM((slides, 32, chans), F32), shape((chans, chans), BF16)],
-        (prods, point, depth_weight),
+        (prods, point, taps),
         "finish",
         36 * chans * chans,
         8,
-        [vmem((slides, 32, chans), F32), dma],
+        [vmem((slides, 32, chans), F32), vmem((2, chans, chans // 2), F32), dma],
         ([IN_VMEM] * 3, [hbm, IN_VMEM]),
     )
     got = swapped(parts, "slide")
 
-    early, step = 40, 8
+    early, step = 32, 8
 
     def scratch(count):
         return [
             *buffers(count),
             vmem((count, cols, chans), BF16),
-            dma((1,)),
-            dma((4,)),
-            dma,
+            dma((5,)),
         ]
 
     half, weights, done = whole(
@@ -390,7 +446,7 @@
             shape((3, chans, 3 * chans), BF16),
             shape((8, 128), F32),
         ],
-        (*halo, point, depth_weight),
+        (*halo, point, taps),
         "back_one",
         18 * macs * early // rows,
         40,
@@ -410,7 +466,7 @@
         32,
         scratch(rows - early),
         ([*halo_specs, IN_VMEM, hbm], [hbm]),
-        {6: 0},
+        {4: 0},
     )
     depth_grad, point_grad = whole(
         functools.partial(third, scale),
@@ -424,16 +480,16 @@
 
 
 def solution(mesh):
-    placed = (
-        P("slide", "row", "col", None),
-        P("slide", "row", "col", None),
-        P(),
-        P(("slide", "row", "col"), None),
-    )
+    slides, rows, cols = (mesh.shape[a] for a in ("slide", "row", "col"))
+    fine = jax.sharding.Mesh(
+        mesh.devices.reshape(slides, rows, cols // 2, 2), ("slide", "row", "half", "pair")
+    )
+    tiles = P("slide", "row", ("half", "pair"), None)
+    lines = P(("slide", "row", "half", "pair"), None)
     return jax.shard_map(
         on_device,
-        mesh=mesh,
-        in_specs=placed,
-        out_specs=(P("slide", "row", "col", None), P(("slide", "row", "col"), None), P()),
+        mesh=fine,
+        in_specs=(tiles, tiles, P(), lines),
+        out_specs=(tiles, lines, P()),
         check_vma=False,
     )

time: 90.5 us -> 80.9 us (0.89)
  starting transfers between devices: 46.3 us -> 39.4 us
  waiting for transfers between devices: 6.55 us -> 5.38 us
    ppermute x4, starting transfers between devices: 17.3 us -> 13.7 us  [across(): return (lax.ppermute(near, axis, pairs), lax.ppermute(far, axis, others))]
    all_to_all x3, starting transfers between devices: 29 us -> 25.8 us  [swapped(): return lax.all_to_all(x, axes, 0, 0, tiled=True)]
    ppermute x4, waiting for transfers between devices: 3.89 us -> 1.01 us  [across(): return (lax.ppermute(near, axis, pairs), lax.ppermute(far, axis, others))]
    all_to_all x3, waiting for transfers between devices: 2.66 us -> 4.36 us  [swapped(): return lax.all_to_all(x, axes, 0, 0, tiled=True)]
  transfers between devices with their start and end apart: 7 -> 7, of which waited for: 4 -> 4; matrix products, arithmetic and copies ran while one was open for 0% -> 0% of each run, Pallas kernels for 33% -> 35%
where the time goes in v3:
time: 80.9 us; the launch traced here: 80.3 us
  starting transfers between devices  39.4 us (49%)
  Pallas kernels  34.1 us (42%)
  waiting for transfers between devices  5.38 us (7%)
    pallas_call x8, Pallas kernels, whole(): pl.pallas_call(body, out_shape=outs, in_specs=ins, out_specs=outs_at, scr...  34.1 us
    all_to_all x3, starting transfers between devices, swapped(): return lax.all_to_all(x, axes, 0, 0, tiled=True)  25.8 us
    ppermute x4, starting transfers between devices, across(): return (lax.ppermute(near, axis, pairs), lax.ppermute(far, axis, others))  13.7 us
    all_to_all x3, waiting for transfers between devices, swapped(): return lax.all_to_all(x, axes, 0, 0, tiled=True)  4.36 us
  transfers between devices with their start and end apart: 7, of which 4 were waited for; matrix products, arithmetic and copies ran while one was open for 0% of the time, Pallas kernels for 35%

profile of v3, /device:TPU:1, one launch (start us, length us, event | category | flops | bytes accessed | tf_op | source)
XLA Modules:
  0.0 80.3 jit_solution(2336240255272591504)
XLA Ops:
  0.6 1.3 %prepare.1 = (bf16[2,128,256]{2,1,0:T(8,128)(2,1)S(1)}, bf16[2,128,256]{2,1,0:T(8,128)(2,1)S(1)}, bf16[65,2,256]{2,1,0:T(2,128)(2,1)S(1)}, bf16[65,2,256]{2,1,0:T(2,128)(2,1)S(1)}, bf16[9,256]{1,0:T(8,128)(2,1)S(1)}) custom-call(bf16[1,256]{1,0:T(2,128)(2,1)} %weight.1, bf16[9,256]{1,0:T(8,128)(2,1)} %taps.1, bf16[64,128,256]{2,1,0:T(8,128)(2,1)} %bitcast.3), custom_call_target="tpu_custom_call" | custom-call | flops 1048576 | bytes 4599296 | tf_op jit(solution)/shard_map/prepare/pallas_call | solution.py:19
  1.9 2.6 %collective-permute-start = (bf16[65,2,256]{2,1,0:T(2,128)(2,1)S(1)}, bf16[65,2,256]{2,1,0:T(2,128)(2,1)S(1)}, u32[]{:S(2)}, u32[]{:S(2)}) collective-permute-start(bf16[65,2,256]{2,1,0:T(2,128)(2,1)S(1)} %get-tuple-element.23.mine), channel_id=1, source_target_pairs={{0,1},{1,0},{2,3},{3,2},{4,5},{5,4},{6,7},{7,6},{8,9},{9,8},{10,11... | collective-permute-start | bytes 199688 | tf_op jit(solution)/shard_map/ppermute | solution.py:341
  4.5 0.7 collective-permute-start.1
  5.2 1.0 %collective-permute-done.near = bf16[65,2,256]{2,1,0:T(2,128)(2,1)S(1)} collective-permute-done((bf16[65,2,256]{2,1,0:T(2,128)(2,1)S(1)}, bf16[65,2,256]{2,1,0:T(2,128)(2,1)S(1)}, u32[]{:S(2)}, u32[]{:S(2)}) %collective-permute-start) | collective-permute-done | bytes 66592 | tf_op jit(solution)/shard_map/ppermute | solution.py:341
  6.2 0.0 collective-permute-done.1.far
  6.2 1.4 %ends.1 = (bf16[128,2,256]{2,1,0:T(2,128)(2,1)}, bf16[2,136,256]{2,1,0:T(8,128)(2,1)S(1)}, bf16[2,136,256]{2,1,0:T(8,128)(2,1)S(1)}, bf16[64,2,256]{2,1,0:T(2,128)(2,1)}, bf16[64,2,256]{2,1,0:T(2,128)(2,1)}) custom-call(bf16[65,2,256]{2,1,0:T(2,128)(2,1)S(1)} %get-tuple-element.23.mine, bf16[2,128,256]{2,1,0:T(8,128)(2,1)S(1)} %get-tuple-element.24.top, ...), custom_call_target="tpu_custom_call" | custom-call | flops 1024 | bytes 1002496 | tf_op jit(solution)/shard_map/ends/pallas_call | solution.py:19
  7.6 3.5 %collective-permute-start.2 = (bf16[2,136,256]{2,1,0:T(8,128)(2,1)S(1)}, bf16[2,136,256]{2,1,0:T(8,128)(2,1)S(1)}, u32[]{:S(2)}, u32[]{:S(2)}) collective-permute-start(bf16[2,136,256]{2,1,0:T(8,128)(2,1)S(1)} %get-tuple-element.27), channel_id=1, source_target_pairs={{0,4},{4,0},{8,12},{12,8},{1,5},{5,1},{9,13},{13,9},{2,6},{6,2},{1... | collective-permute-start | bytes 417800 | tf_op jit(solution)/shard_map/ppermute | solution.py:341
  11.1 7.0 %collective-permute-start.3 = (bf16[2,136,256]{2,1,0:T(8,128)(2,1)S(1)}, bf16[2,136,256]{2,1,0:T(8,128)(2,1)S(1)}, u32[]{:S(2)}, u32[]{:S(2)}) collective-permute-start(bf16[2,136,256]{2,1,0:T(8,128)(2,1)S(1)} %get-tuple-element.28), channel_id=1, source_target_pairs={{4,8},{8,4},{5,9},{9,5},{6,10},{10,6},{7,11},{11,7},{20,24},{24,20... | collective-permute-start | bytes 417800 | tf_op jit(solution)/shard_map/ppermute | solution.py:341
  18.1 12.2 %all-to-all-start = ((bf16[128,2,256]{2,1,0:T(2,128)(2,1)}), bf16[128,2,256]{2,1,0:T(2,128)(2,1)S(1)}, u32[]{:S(2)}, u32[]{:S(2)}) async-start(bf16[128,2,256]{2,1,0:T(2,128)(2,1)} %get-tuple-element.34), calls=%async_computation | async-start | bytes 262144 | tf_op jit(solution)/shard_map/all_to_all | solution.py:345
  30.3 0.0 collective-permute-done.2.near_hbm
  30.3 0.0 copy-start
  30.3 0.0 collective-permute-done.3.far_hbm
  30.3 0.0 copy-start.1
  30.3 0.7 copy-done.1
  31.0 0.0 copy-done
  31.0 10.0 %products.1 = (f32[4,256,768]{2,1,0:T(8,128)S(1)}, bf16[2,2,128,256]{3,2,1,0:T(8,128)(2,1)}, bf16[2,68,2,256]{3,2,1,0:T(2,128)(2,1)}) custom-call(bf16[64,128,256]{2,1,0:T(8,128)(2,1)} %bitcast.7, bf16[64,128,256]{2,1,0:T(8,128)(2,1)} %bitcast.4, bf16[2,136,256]{2,1,0:T(8,128)(2,1)} %copy-done, bf16[2,136,256]{2,1,0:T(8,128)(2,1)} %copy-done.1, ...), custom_call_target="tpu_custom_call" | custom-call | flops 6442450944 | bytes 12345344 | tf_op jit(solution)/shard_map/products/pallas_call | solution.py:19
  41.0 2.0 %all-to-all-done.point = bf16[128,2,256]{2,1,0:T(2,128)(2,1)S(1)} async-done(((bf16[128,2,256]{2,1,0:T(2,128)(2,1)}), bf16[128,2,256]{2,1,0:T(2,128)(2,1)S(1)}, u32[]{:S(2)}, u32[]{:S(2)}) %all-to-all-start) | async-done | bytes 131104 | tf_op jit(solution)/shard_map/all_to_all | solution.py:345
  43.0 2.0 %finish.1 = (f32[16,32,256]{2,1,0:T(8,128)}, bf16[256,256]{1,0:T(8,128)(2,1)S(1)}) custom-call(f32[4,256,768]{2,1,0:T(8,128)S(1)} %get-tuple-element.33.prods, bf16[128,2,256]{2,1,0:T(2,128)(2,1)S(1)} %all-to-all-done.point, bf16[9,256]{1,0:T(8,128)(2,1)S(1)} %get-tuple-element.35.taps), custom_call_target="tpu_custom_call" | custom-call | flops 2359296 | bytes 3936768 | tf_op jit(solution)/shard_map/finish/pallas_call | solution.py:19
  45.1 5.2 %all-to-all-start.1 = ((f32[16,32,256]{2,1,0:T(8,128)}), f32[16,32,256]{2,1,0:T(8,128)S(1)}, u32[]{:S(2)}, u32[]{:S(2)}) async-start(f32[16,32,256]{2,1,0:T(8,128)} %get-tuple-element.39), calls=%async_computation.1 | async-start | bytes 1048576 | tf_op jit(solution)/shard_map/all_to_all | solution.py:345
  50.2 8.9 %back_one.1 = (bf16[64,128,256]{2,1,0:T(8,128)(2,1)}, bf16[3,256,768]{2,1,0:T(8,128)(2,1)S(1)}, f32[8,128]{1,0:T(8,128)S(1)}) custom-call(bf16[64,128,256]{2,1,0:T(8,128)(2,1)} %bitcast.5, bf16[2,2,128,256]{3,2,1,0:T(8,128)(2,1)} %get-tuple-element.31.rim, bf16[2,68,2,256]{3,2,1,0:T(2,128)(2,1)} %get-tuple-element.32.pair_hbm, ...), custom_call_target="tpu_custom_call" | custom-call | flops 4831838208 | bytes 10109440 | tf_op jit(solution)/shard_map/back_one/pallas_call | solution.py:19
  59.2 1.8 %all-to-all-done.1.got = f32[16,32,256]{2,1,0:T(8,128)S(1)} async-done(((f32[16,32,256]{2,1,0:T(8,128)}), f32[16,32,256]{2,1,0:T(8,128)S(1)}, u32[]{:S(2)}, u32[]{:S(2)}) %all-to-all-start.1) | async-done | bytes 524320 | tf_op jit(solution)/shard_map/all_to_all | solution.py:345
  61.0 0.7 second.1
  61.7 8.4 %all-to-all-start.2 = ((f32[16,16,256]{2,1,0:T(8,128)}), f32[16,16,256]{2,1,0:T(8,128)S(1)}, u32[]{:S(2)}, u32[]{:S(2)}) async-start(f32[16,16,256]{2,1,0:T(8,128)} %second.1), calls=%async_computation.2 | async-start | bytes 524288 | tf_op jit(solution)/shard_map/all_to_all | solution.py:345
  70.1 9.0 %back_two.1 = bf16[64,128,256]{2,1,0:T(8,128)(2,1)} custom-call(bf16[64,128,256]{2,1,0:T(8,128)(2,1)} %bitcast.6, bf16[2,2,128,256]{3,2,1,0:T(8,128)(2,1)} %get-tuple-element.31.rim, bf16[2,68,2,256]{3,2,1,0:T(2,128)(2,1)} %get-tuple-element.32.pair_hbm, bf16[3,256,768]{2,1,0:T(8,128)(2,1)S(1)} %get-tuple-element.37.weights, ...), custom_call_target="tpu_custom_call", output_to_operand_aliasing={{}: (4, {})} | custom-call | flops 4831838208 | bytes 14163968 | tf_op jit(solution)/shard_map/back_two/pallas_call | solution.py:19
  79.1 0.6 all-to-all-done.2.got
  79.7 0.6 third.1
Async XLA Ops:
  1.9 4.2 %collective-permute-start = (bf16[65,2,256]{2,1,0:T(2,128)(2,1)S(1)}, bf16[65,2,256]{2,1,0:T(2,128)(2,1)S(1)}, u32[]{:S(2)}, u32[]{:S(2)}) collective-permute-start(bf16[65,2,256]{2,1,0:T(2,128)(2,1)S(1)} %get-tuple-element.23.mine), channel_id=1, source_target_pairs={{0,1},{1,0},{2,3},{3,2},{4,5},{5,4},{6,7},{7,6},{8,9},{9,8},{10,11... | collective-permute-start | bytes 199688 | tf_op jit(solution)/shard_map/ppermute | solution.py:341
  4.5 1.7 %collective-permute-start.1 = (bf16[65,2,256]{2,1,0:T(2,128)(2,1)S(1)}, bf16[65,2,256]{2,1,0:T(2,128)(2,1)S(1)}, u32[]{:S(2)}, u32[]{:S(2)}) collective-permute-start(bf16[65,2,256]{2,1,0:T(2,128)(2,1)S(1)} %get-tuple-element.26), channel_id=1, source_target_pairs={{1,2},{2,1},{5,6},{6,5},{9,10},{10,9},{13,14},{14,13},{17,18},{18,... | collective-permute-start | bytes 199688 | tf_op jit(solution)/shard_map/ppermute | solution.py:341
  7.6 22.7 %collective-permute-start.2 = (bf16[2,136,256]{2,1,0:T(8,128)(2,1)S(1)}, bf16[2,136,256]{2,1,0:T(8,128)(2,1)S(1)}, u32[]{:S(2)}, u32[]{:S(2)}) collective-permute-start(bf16[2,136,256]{2,1,0:T(8,128)(2,1)S(1)} %get-tuple-element.27), channel_id=1, source_target_pairs={{0,4},{4,0},{8,12},{12,8},{1,5},{5,1},{9,13},{13,9},{2,6},{6,2},{1... | collective-permute-start | bytes 417800 | tf_op jit(solution)/shard_map/ppermute | solution.py:341
  11.1 19.2 %collective-permute-start.3 = (bf16[2,136,256]{2,1,0:T(8,128)(2,1)S(1)}, bf16[2,136,256]{2,1,0:T(8,128)(2,1)S(1)}, u32[]{:S(2)}, u32[]{:S(2)}) collective-permute-start(bf16[2,136,256]{2,1,0:T(8,128)(2,1)S(1)} %get-tuple-element.28), channel_id=1, source_target_pairs={{4,8},{8,4},{5,9},{9,5},{6,10},{10,6},{7,11},{11,7},{20,24},{24,20... | collective-permute-start | bytes 417800 | tf_op jit(solution)/shard_map/ppermute | solution.py:341
  18.1 24.9 %all-to-all-start = ((bf16[128,2,256]{2,1,0:T(2,128)(2,1)}), bf16[128,2,256]{2,1,0:T(2,128)(2,1)S(1)}, u32[]{:S(2)}, u32[]{:S(2)}) async-start(bf16[128,2,256]{2,1,0:T(2,128)(2,1)} %get-tuple-element.34), calls=%async_computation | async-start | bytes 262144 | tf_op jit(solution)/shard_map/all_to_all | solution.py:345
  30.3 0.7 copy-start
  30.3 0.7 copy-start.1
  45.1 15.9 %all-to-all-start.1 = ((f32[16,32,256]{2,1,0:T(8,128)}), f32[16,32,256]{2,1,0:T(8,128)S(1)}, u32[]{:S(2)}, u32[]{:S(2)}) async-start(f32[16,32,256]{2,1,0:T(8,128)} %get-tuple-element.39), calls=%async_computation.1 | async-start | bytes 1048576 | tf_op jit(solution)/shard_map/all_to_all | solution.py:345
  61.7 18.0 %all-to-all-start.2 = ((f32[16,16,256]{2,1,0:T(8,128)}), f32[16,16,256]{2,1,0:T(8,128)S(1)}, u32[]{:S(2)}, u32[]{:S(2)}) async-start(f32[16,16,256]{2,1,0:T(8,128)} %second.1), calls=%async_computation.2 | async-start | bytes 524288 | tf_op jit(solution)/shard_map/all_to_all | solution.py:345

commit v4 on v3

--- a/solution.py
+++ b/solution.py
@@ -119,7 +119,7 @@
             [pair[0, begin + i], row[: cols - 2]], axis=0
         )
 
-    each(low, high, put)
+    each(low // 4, high // 4, lambda g: [put(4 * g + u) for u in range(4)])
 
 
 def four_products(feat, wide, first, fold):
@@ -236,8 +236,8 @@
     share = chans // groups
     tap_rows = sums.T[:16]
     for s in range(groups):
-        stage[s, :share] = acc[s * share : (s + 1) * share]
-        stage[s, share:] = tap_rows
+        stage[s, :share] = acc[s * share : (s + 1) * share].astype(BF16)
+        stage[s, share:] = tap_rows.astype(BF16)
     copy = pltpu.make_async_copy(stage, out, sem)
     copy.start()
     copy.wait()
@@ -245,9 +245,9 @@
 
 def second(got, done, out):
     del done
-    total = got[0]
+    total = got[0].astype(F32)
     for s in range(1, got.shape[0]):
-        total = total + got[s]
+        total = total + got[s].astype(F32)
     rows = total.shape[0] // 2
     tap = total[rows:]
     sub = lax.broadcasted_iota(jnp.int32, tap.shape, 0)
@@ -420,12 +420,12 @@
     halo_specs = [hbm] * 3
     parts, point = whole(
         finish,
-        [pltpu.HBM((slides, 32, chans), F32), shape((chans, chans), BF16)],
+        [pltpu.HBM((slides, 32, chans), BF16), shape((chans, chans), BF16)],
         (prods, point, taps),
         "finish",
         36 * chans * chans,
         8,
-        [vmem((slides, 32, chans), F32), vmem((2, chans, chans // 2), F32), dma],
+        [vmem((slides, 32, chans), BF16), vmem((2, chans, chans // 2), F32), dma],
         ([IN_VMEM] * 3, [hbm, IN_VMEM]),
     )
     got = swapped(parts, "slide")

time: 80.9 us -> 78.3 us (0.968)
  waiting for transfers between devices: 5.38 us -> 3.69 us
  starting transfers between devices: 39.4 us -> 38.4 us
    all_to_all x3, waiting for transfers between devices: 4.36 us -> 2.68 us  [swapped(): return lax.all_to_all(x, axes, 0, 0, tiled=True)]
    all_to_all x3, starting transfers between devices: 25.8 us -> 24.7 us  [swapped(): return lax.all_to_all(x, axes, 0, 0, tiled=True)]
  transfers between devices with their start and end apart: 7 -> 7, of which waited for: 4 -> 3; matrix products, arithmetic and copies ran while one was open for 0% -> 0% of each run, Pallas kernels for 35% -> 36%
where the time goes in v4:
time: 78.3 us; the launch traced here: 77.4 us
  starting transfers between devices  38.4 us (49%)
  Pallas kernels  33.8 us (43%)
  waiting for transfers between devices  3.69 us (5%)
    pallas_call x8, Pallas kernels, whole(): pl.pallas_call(body, out_shape=outs, in_specs=ins, out_specs=outs_at, scr...  33.8 us
    all_to_all x3, starting transfers between devices, swapped(): return lax.all_to_all(x, axes, 0, 0, tiled=True)  24.7 us
    ppermute x4, starting transfers between devices, across(): return (lax.ppermute(near, axis, pairs), lax.ppermute(far, axis, others))  13.7 us
    all_to_all x3, waiting for transfers between devices, swapped(): return lax.all_to_all(x, axes, 0, 0, tiled=True)  2.68 us
  transfers between devices with their start and end apart: 7, of which 3 were waited for; matrix products, arithmetic and copies ran while one was open for 0% of the time, Pallas kernels for 36%

profile of v4, /device:TPU:1, one launch (start us, length us, event | category | flops | bytes accessed | tf_op | source)
XLA Modules:
  0.0 77.4 jit_solution(4474455541777036578)
XLA Ops:
  0.6 1.3 %prepare.1 = (bf16[2,128,256]{2,1,0:T(8,128)(2,1)S(1)}, bf16[2,128,256]{2,1,0:T(8,128)(2,1)S(1)}, bf16[65,2,256]{2,1,0:T(2,128)(2,1)S(1)}, bf16[65,2,256]{2,1,0:T(2,128)(2,1)S(1)}, bf16[9,256]{1,0:T(8,128)(2,1)S(1)}) custom-call(bf16[1,256]{1,0:T(2,128)(2,1)} %weight.1, bf16[9,256]{1,0:T(8,128)(2,1)} %taps.1, bf16[64,128,256]{2,1,0:T(8,128)(2,1)} %bitcast.3), custom_call_target="tpu_custom_call" | custom-call | flops 1048576 | bytes 4599296 | tf_op jit(solution)/shard_map/prepare/pallas_call | solution.py:19
  1.9 2.6 %collective-permute-start = (bf16[65,2,256]{2,1,0:T(2,128)(2,1)S(1)}, bf16[65,2,256]{2,1,0:T(2,128)(2,1)S(1)}, u32[]{:S(2)}, u32[]{:S(2)}) collective-permute-start(bf16[65,2,256]{2,1,0:T(2,128)(2,1)S(1)} %get-tuple-element.23.mine), channel_id=1, source_target_pairs={{0,1},{1,0},{2,3},{3,2},{4,5},{5,4},{6,7},{7,6},{8,9},{9,8},{10,11... | collective-permute-start | bytes 199688 | tf_op jit(solution)/shard_map/ppermute | solution.py:341
  4.5 0.7 collective-permute-start.1
  5.2 1.0 %collective-permute-done.near = bf16[65,2,256]{2,1,0:T(2,128)(2,1)S(1)} collective-permute-done((bf16[65,2,256]{2,1,0:T(2,128)(2,1)S(1)}, bf16[65,2,256]{2,1,0:T(2,128)(2,1)S(1)}, u32[]{:S(2)}, u32[]{:S(2)}) %collective-permute-start) | collective-permute-done | bytes 66592 | tf_op jit(solution)/shard_map/ppermute | solution.py:341
  6.2 0.0 collective-permute-done.1.far
  6.2 1.4 %ends.1 = (bf16[128,2,256]{2,1,0:T(2,128)(2,1)}, bf16[2,136,256]{2,1,0:T(8,128)(2,1)S(1)}, bf16[2,136,256]{2,1,0:T(8,128)(2,1)S(1)}, bf16[64,2,256]{2,1,0:T(2,128)(2,1)}, bf16[64,2,256]{2,1,0:T(2,128)(2,1)}) custom-call(bf16[65,2,256]{2,1,0:T(2,128)(2,1)S(1)} %get-tuple-element.23.mine, bf16[2,128,256]{2,1,0:T(8,128)(2,1)S(1)} %get-tuple-element.24.top, ...), custom_call_target="tpu_custom_call" | custom-call | flops 1024 | bytes 1002496 | tf_op jit(solution)/shard_map/ends/pallas_call | solution.py:19
  7.6 3.5 %collective-permute-start.2 = (bf16[2,136,256]{2,1,0:T(8,128)(2,1)S(1)}, bf16[2,136,256]{2,1,0:T(8,128)(2,1)S(1)}, u32[]{:S(2)}, u32[]{:S(2)}) collective-permute-start(bf16[2,136,256]{2,1,0:T(8,128)(2,1)S(1)} %get-tuple-element.27), channel_id=1, source_target_pairs={{0,4},{4,0},{8,12},{12,8},{1,5},{5,1},{9,13},{13,9},{2,6},{6,2},{1... | collective-permute-start | bytes 417800 | tf_op jit(solution)/shard_map/ppermute | solution.py:341
  11.1 7.0 %collective-permute-start.3 = (bf16[2,136,256]{2,1,0:T(8,128)(2,1)S(1)}, bf16[2,136,256]{2,1,0:T(8,128)(2,1)S(1)}, u32[]{:S(2)}, u32[]{:S(2)}) collective-permute-start(bf16[2,136,256]{2,1,0:T(8,128)(2,1)S(1)} %get-tuple-element.28), channel_id=1, source_target_pairs={{4,8},{8,4},{5,9},{9,5},{6,10},{10,6},{7,11},{11,7},{20,24},{24,20... | collective-permute-start | bytes 417800 | tf_op jit(solution)/shard_map/ppermute | solution.py:341
  18.1 12.2 %all-to-all-start = ((bf16[128,2,256]{2,1,0:T(2,128)(2,1)}), bf16[128,2,256]{2,1,0:T(2,128)(2,1)S(1)}, u32[]{:S(2)}, u32[]{:S(2)}) async-start(bf16[128,2,256]{2,1,0:T(2,128)(2,1)} %get-tuple-element.34), calls=%async_computation | async-start | bytes 262144 | tf_op jit(solution)/shard_map/all_to_all | solution.py:345
  30.3 0.0 collective-permute-done.2.near_hbm
  30.3 0.0 copy-start
  30.3 0.0 collective-permute-done.3.far_hbm
  30.3 0.0 copy-start.1
  30.3 0.7 copy-done.1
  31.0 0.0 copy-done
  31.0 10.0 %products.1 = (f32[4,256,768]{2,1,0:T(8,128)S(1)}, bf16[2,2,128,256]{3,2,1,0:T(8,128)(2,1)}, bf16[2,68,2,256]{3,2,1,0:T(2,128)(2,1)}) custom-call(bf16[64,128,256]{2,1,0:T(8,128)(2,1)} %bitcast.7, bf16[64,128,256]{2,1,0:T(8,128)(2,1)} %bitcast.4, bf16[2,136,256]{2,1,0:T(8,128)(2,1)} %copy-done, bf16[2,136,256]{2,1,0:T(8,128)(2,1)} %copy-done.1, ...), custom_call_target="tpu_custom_call" | custom-call | flops 6442450944 | bytes 12345344 | tf_op jit(solution)/shard_map/products/pallas_call | solution.py:19
  41.0 2.0 %all-to-all-done.point = bf16[128,2,256]{2,1,0:T(2,128)(2,1)S(1)} async-done(((bf16[128,2,256]{2,1,0:T(2,128)(2,1)}), bf16[128,2,256]{2,1,0:T(2,128)(2,1)S(1)}, u32[]{:S(2)}, u32[]{:S(2)}) %all-to-all-start) | async-done | bytes 131104 | tf_op jit(solution)/shard_map/all_to_all | solution.py:345
  43.0 1.9 %finish.1 = (bf16[16,32,256]{2,1,0:T(8,128)(2,1)}, bf16[256,256]{1,0:T(8,128)(2,1)S(1)}) custom-call(f32[4,256,768]{2,1,0:T(8,128)S(1)} %get-tuple-element.33.prods, bf16[128,2,256]{2,1,0:T(2,128)(2,1)S(1)} %all-to-all-done.point, bf16[9,256]{1,0:T(8,128)(2,1)S(1)} %get-tuple-element.35.taps), custom_call_target="tpu_custom_call" | custom-call | flops 2359296 | bytes 3674624 | tf_op jit(solution)/shard_map/finish/pallas_call | solution.py:19
  44.9 5.1 %all-to-all-start.1 = ((bf16[16,32,256]{2,1,0:T(8,128)(2,1)}), bf16[16,32,256]{2,1,0:T(8,128)(2,1)S(1)}, u32[]{:S(2)}, u32[]{:S(2)}) async-start(bf16[16,32,256]{2,1,0:T(8,128)(2,1)} %get-tuple-element.39), calls=%async_computation.1 | async-start | bytes 524288 | tf_op jit(solution)/shard_map/all_to_all | solution.py:345
  50.1 8.9 %back_one.1 = (bf16[64,128,256]{2,1,0:T(8,128)(2,1)}, bf16[3,256,768]{2,1,0:T(8,128)(2,1)S(1)}, f32[8,128]{1,0:T(8,128)S(1)}) custom-call(bf16[64,128,256]{2,1,0:T(8,128)(2,1)} %bitcast.5, bf16[2,2,128,256]{3,2,1,0:T(8,128)(2,1)} %get-tuple-element.31.rim, bf16[2,68,2,256]{3,2,1,0:T(2,128)(2,1)} %get-tuple-element.32.pair_hbm, ...), custom_call_target="tpu_custom_call" | custom-call | flops 4831838208 | bytes 10109440 | tf_op jit(solution)/shard_map/back_one/pallas_call | solution.py:19
  59.0 0.0 all-to-all-done.1.got
  59.0 0.8 second.1
  59.8 7.4 %all-to-all-start.2 = ((f32[16,16,256]{2,1,0:T(8,128)}), f32[16,16,256]{2,1,0:T(8,128)S(1)}, u32[]{:S(2)}, u32[]{:S(2)}) async-start(f32[16,16,256]{2,1,0:T(8,128)} %second.1), calls=%async_computation.2 | async-start | bytes 524288 | tf_op jit(solution)/shard_map/all_to_all | solution.py:345
  67.2 8.9 %back_two.1 = bf16[64,128,256]{2,1,0:T(8,128)(2,1)} custom-call(bf16[64,128,256]{2,1,0:T(8,128)(2,1)} %bitcast.6, bf16[2,2,128,256]{3,2,1,0:T(8,128)(2,1)} %get-tuple-element.31.rim, bf16[2,68,2,256]{3,2,1,0:T(2,128)(2,1)} %get-tuple-element.32.pair_hbm, bf16[3,256,768]{2,1,0:T(8,128)(2,1)S(1)} %get-tuple-element.37.weights, ...), custom_call_target="tpu_custom_call", output_to_operand_aliasing={{}: (4, {})} | custom-call | flops 4831838208 | bytes 14163968 | tf_op jit(solution)/shard_map/back_two/pallas_call | solution.py:19
  76.1 0.7 all-to-all-done.2.got
  76.7 0.6 third.1
Async XLA Ops:
  1.9 4.2 %collective-permute-start = (bf16[65,2,256]{2,1,0:T(2,128)(2,1)S(1)}, bf16[65,2,256]{2,1,0:T(2,128)(2,1)S(1)}, u32[]{:S(2)}, u32[]{:S(2)}) collective-permute-start(bf16[65,2,256]{2,1,0:T(2,128)(2,1)S(1)} %get-tuple-element.23.mine), channel_id=1, source_target_pairs={{0,1},{1,0},{2,3},{3,2},{4,5},{5,4},{6,7},{7,6},{8,9},{9,8},{10,11... | collective-permute-start | bytes 199688 | tf_op jit(solution)/shard_map/ppermute | solution.py:341
  4.5 1.7 %collective-permute-start.1 = (bf16[65,2,256]{2,1,0:T(2,128)(2,1)S(1)}, bf16[65,2,256]{2,1,0:T(2,128)(2,1)S(1)}, u32[]{:S(2)}, u32[]{:S(2)}) collective-permute-start(bf16[65,2,256]{2,1,0:T(2,128)(2,1)S(1)} %get-tuple-element.26), channel_id=1, source_target_pairs={{1,2},{2,1},{5,6},{6,5},{9,10},{10,9},{13,14},{14,13},{17,18},{18,... | collective-permute-start | bytes 199688 | tf_op jit(solution)/shard_map/ppermute | solution.py:341
  7.6 22.7 %collective-permute-start.2 = (bf16[2,136,256]{2,1,0:T(8,128)(2,1)S(1)}, bf16[2,136,256]{2,1,0:T(8,128)(2,1)S(1)}, u32[]{:S(2)}, u32[]{:S(2)}) collective-permute-start(bf16[2,136,256]{2,1,0:T(8,128)(2,1)S(1)} %get-tuple-element.27), channel_id=1, source_target_pairs={{0,4},{4,0},{8,12},{12,8},{1,5},{5,1},{9,13},{13,9},{2,6},{6,2},{1... | collective-permute-start | bytes 417800 | tf_op jit(solution)/shard_map/ppermute | solution.py:341
  11.1 19.2 %collective-permute-start.3 = (bf16[2,136,256]{2,1,0:T(8,128)(2,1)S(1)}, bf16[2,136,256]{2,1,0:T(8,128)(2,1)S(1)}, u32[]{:S(2)}, u32[]{:S(2)}) collective-permute-start(bf16[2,136,256]{2,1,0:T(8,128)(2,1)S(1)} %get-tuple-element.28), channel_id=1, source_target_pairs={{4,8},{8,4},{5,9},{9,5},{6,10},{10,6},{7,11},{11,7},{20,24},{24,20... | collective-permute-start | bytes 417800 | tf_op jit(solution)/shard_map/ppermute | solution.py:341
  18.1 24.9 %all-to-all-start = ((bf16[128,2,256]{2,1,0:T(2,128)(2,1)}), bf16[128,2,256]{2,1,0:T(2,128)(2,1)S(1)}, u32[]{:S(2)}, u32[]{:S(2)}) async-start(bf16[128,2,256]{2,1,0:T(2,128)(2,1)} %get-tuple-element.34), calls=%async_computation | async-start | bytes 262144 | tf_op jit(solution)/shard_map/all_to_all | solution.py:345
  30.3 0.7 copy-start
  30.3 0.7 copy-start.1
  44.9 14.1 %all-to-all-start.1 = ((bf16[16,32,256]{2,1,0:T(8,128)(2,1)}), bf16[16,32,256]{2,1,0:T(8,128)(2,1)S(1)}, u32[]{:S(2)}, u32[]{:S(2)}) async-start(bf16[16,32,256]{2,1,0:T(8,128)(2,1)} %get-tuple-element.39), calls=%async_computation.1 | async-start | bytes 524288 | tf_op jit(solution)/shard_map/all_to_all | solution.py:345
  59.8 17.0 %all-to-all-start.2 = ((f32[16,16,256]{2,1,0:T(8,128)}), f32[16,16,256]{2,1,0:T(8,128)S(1)}, u32[]{:S(2)}, u32[]{:S(2)}) async-start(f32[16,16,256]{2,1,0:T(8,128)} %second.1), calls=%async_computation.2 | async-start | bytes 524288 | tf_op jit(solution)/shard_map/all_to_all | solution.py:345

commit v5 on v4

--- a/solution.py
+++ b/solution.py
@@ -252,13 +252,13 @@
     tap = total[rows:]
     sub = lax.broadcasted_iota(jnp.int32, tap.shape, 0)
     for r in range(out.shape[0]):
-        out[r] = jnp.where(sub == 9, total[r : r + 1], tap)
+        out[r] = jnp.where(sub == 9, total[r : r + 1], tap).astype(BF16)
 
 
 def third(scale, got, taps, row):
-    total = got[0]
+    total = got[0].astype(F32)
     for s in range(1, got.shape[0]):
-        total = total + got[s]
+        total = total + got[s].astype(F32)
     total = total * scale
     taps[...] = total[:9]
     row[...] = total[9:10]
@@ -454,7 +454,7 @@
         ([*halo_specs, IN_VMEM, IN_VMEM], [hbm, IN_VMEM, IN_VMEM]),
     )
     (parts,) = whole(
-        second, [shape((places, 16, chans), F32)], (got, done), "second", 1 << 20, 4
+        second, [shape((places, 16, chans), BF16)], (got, done), "second", 1 << 20, 4
     )
     got = swapped(parts, place)
     (feature_grad,) = whole(

time: 78.3 us -> 77.1 us (0.985)
  transfers between devices with their start and end apart: 7 -> 7, of which waited for: 3 -> 2; matrix products, arithmetic and copies ran while one was open for 0% -> 0% of each run, Pallas kernels for 36% -> 36%
where the time goes in v5:
time: 77.1 us; the launch traced here: 76.7 us
  starting transfers between devices  38.4 us (50%)
  Pallas kernels  33.8 us (44%)
  waiting for transfers between devices  3.02 us (4%)
    pallas_call x8, Pallas kernels, whole(): pl.pallas_call(body, out_shape=outs, in_specs=ins, out_specs=outs_at, scr...  33.8 us
    all_to_all x3, starting transfers between devices, swapped(): return lax.all_to_all(x, axes, 0, 0, tiled=True)  24.7 us
    ppermute x4, starting transfers between devices, across(): return (lax.ppermute(near, axis, pairs), lax.ppermute(far, axis, others))  13.7 us
    all_to_all x3, waiting for transfers between devices, swapped(): return lax.all_to_all(x, axes, 0, 0, tiled=True)  2.01 us
  transfers between devices with their start and end apart: 7, of which 2 were waited for; matrix products, arithmetic and copies ran while one was open for 0% of the time, Pallas kernels for 36%

profile of v5, /device:TPU:1, one launch (start us, length us, event | category | flops | bytes accessed | tf_op | source)
XLA Modules:
  0.0 76.7 jit_solution(9328874927111512174)
XLA Ops:
  0.6 1.3 %prepare.1 = (bf16[2,128,256]{2,1,0:T(8,128)(2,1)S(1)}, bf16[2,128,256]{2,1,0:T(8,128)(2,1)S(1)}, bf16[65,2,256]{2,1,0:T(2,128)(2,1)S(1)}, bf16[65,2,256]{2,1,0:T(2,128)(2,1)S(1)}, bf16[9,256]{1,0:T(8,128)(2,1)S(1)}) custom-call(bf16[1,256]{1,0:T(2,128)(2,1)} %weight.1, bf16[9,256]{1,0:T(8,128)(2,1)} %taps.1, bf16[64,128,256]{2,1,0:T(8,128)(2,1)} %bitcast.3), custom_call_target="tpu_custom_call" | custom-call | flops 1048576 | bytes 4599296 | tf_op jit(solution)/shard_map/prepare/pallas_call | solution.py:19
  1.9 2.6 %collective-permute-start = (bf16[65,2,256]{2,1,0:T(2,128)(2,1)S(1)}, bf16[65,2,256]{2,1,0:T(2,128)(2,1)S(1)}, u32[]{:S(2)}, u32[]{:S(2)}) collective-permute-start(bf16[65,2,256]{2,1,0:T(2,128)(2,1)S(1)} %get-tuple-element.23.mine), channel_id=1, source_target_pairs={{0,1},{1,0},{2,3},{3,2},{4,5},{5,4},{6,7},{7,6},{8,9},{9,8},{10,11... | collective-permute-start | bytes 199688 | tf_op jit(solution)/shard_map/ppermute | solution.py:341
  4.5 0.7 collective-permute-start.1
  5.2 1.0 %collective-permute-done.near = bf16[65,2,256]{2,1,0:T(2,128)(2,1)S(1)} collective-permute-done((bf16[65,2,256]{2,1,0:T(2,128)(2,1)S(1)}, bf16[65,2,256]{2,1,0:T(2,128)(2,1)S(1)}, u32[]{:S(2)}, u32[]{:S(2)}) %collective-permute-start) | collective-permute-done | bytes 66592 | tf_op jit(solution)/shard_map/ppermute | solution.py:341
  6.2 0.0 collective-permute-done.1.far
  6.2 1.4 %ends.1 = (bf16[128,2,256]{2,1,0:T(2,128)(2,1)}, bf16[2,136,256]{2,1,0:T(8,128)(2,1)S(1)}, bf16[2,136,256]{2,1,0:T(8,128)(2,1)S(1)}, bf16[64,2,256]{2,1,0:T(2,128)(2,1)}, bf16[64,2,256]{2,1,0:T(2,128)(2,1)}) custom-call(bf16[65,2,256]{2,1,0:T(2,128)(2,1)S(1)} %get-tuple-element.23.mine, bf16[2,128,256]{2,1,0:T(8,128)(2,1)S(1)} %get-tuple-element.24.top, ...), custom_call_target="tpu_custom_call" | custom-call | flops 1024 | bytes 1002496 | tf_op jit(solution)/shard_map/ends/pallas_call | solution.py:19
  7.6 3.5 %collective-permute-start.2 = (bf16[2,136,256]{2,1,0:T(8,128)(2,1)S(1)}, bf16[2,136,256]{2,1,0:T(8,128)(2,1)S(1)}, u32[]{:S(2)}, u32[]{:S(2)}) collective-permute-start(bf16[2,136,256]{2,1,0:T(8,128)(2,1)S(1)} %get-tuple-element.27), channel_id=1, source_target_pairs={{0,4},{4,0},{8,12},{12,8},{1,5},{5,1},{9,13},{13,9},{2,6},{6,2},{1... | collective-permute-start | bytes 417800 | tf_op jit(solution)/shard_map/ppermute | solution.py:341
  11.1 7.0 %collective-permute-start.3 = (bf16[2,136,256]{2,1,0:T(8,128)(2,1)S(1)}, bf16[2,136,256]{2,1,0:T(8,128)(2,1)S(1)}, u32[]{:S(2)}, u32[]{:S(2)}) collective-permute-start(bf16[2,136,256]{2,1,0:T(8,128)(2,1)S(1)} %get-tuple-element.28), channel_id=1, source_target_pairs={{4,8},{8,4},{5,9},{9,5},{6,10},{10,6},{7,11},{11,7},{20,24},{24,20... | collective-permute-start | bytes 417800 | tf_op jit(solution)/shard_map/ppermute | solution.py:341
  18.1 12.2 %all-to-all-start = ((bf16[128,2,256]{2,1,0:T(2,128)(2,1)}), bf16[128,2,256]{2,1,0:T(2,128)(2,1)S(1)}, u32[]{:S(2)}, u32[]{:S(2)}) async-start(bf16[128,2,256]{2,1,0:T(2,128)(2,1)} %get-tuple-element.34), calls=%async_computation | async-start | bytes 262144 | tf_op jit(solution)/shard_map/all_to_all | solution.py:345
  30.3 0.0 collective-permute-done.2.near_hbm
  30.3 0.0 copy-start
  30.3 0.0 collective-permute-done.3.far_hbm
  30.3 0.0 copy-start.1
  30.3 0.7 copy-done.1
  31.0 0.0 copy-done
  31.0 10.0 %products.1 = (f32[4,256,768]{2,1,0:T(8,128)S(1)}, bf16[2,2,128,256]{3,2,1,0:T(8,128)(2,1)}, bf16[2,68,2,256]{3,2,1,0:T(2,128)(2,1)}) custom-call(bf16[64,128,256]{2,1,0:T(8,128)(2,1)} %bitcast.7, bf16[64,128,256]{2,1,0:T(8,128)(2,1)} %bitcast.4, bf16[2,136,256]{2,1,0:T(8,128)(2,1)} %copy-done, bf16[2,136,256]{2,1,0:T(8,128)(2,1)} %copy-done.1, ...), custom_call_target="tpu_custom_call" | custom-call | flops 6442450944 | bytes 12345344 | tf_op jit(solution)/shard_map/products/pallas_call | solution.py:19
  41.0 2.0 %all-to-all-done.point = bf16[128,2,256]{2,1,0:T(2,128)(2,1)S(1)} async-done(((bf16[128,2,256]{2,1,0:T(2,128)(2,1)}), bf16[128,2,256]{2,1,0:T(2,128)(2,1)S(1)}, u32[]{:S(2)}, u32[]{:S(2)}) %all-to-all-start) | async-done | bytes 131104 | tf_op jit(solution)/shard_map/all_to_all | solution.py:345
  43.0 1.9 %finish.1 = (bf16[16,32,256]{2,1,0:T(8,128)(2,1)}, bf16[256,256]{1,0:T(8,128)(2,1)S(1)}) custom-call(f32[4,256,768]{2,1,0:T(8,128)S(1)} %get-tuple-element.33.prods, bf16[128,2,256]{2,1,0:T(2,128)(2,1)S(1)} %all-to-all-done.point, bf16[9,256]{1,0:T(8,128)(2,1)S(1)} %get-tuple-element.35.taps), custom_call_target="tpu_custom_call" | custom-call | flops 2359296 | bytes 3674624 | tf_op jit(solution)/shard_map/finish/pallas_call | solution.py:19
  44.9 5.1 %all-to-all-start.1 = ((bf16[16,32,256]{2,1,0:T(8,128)(2,1)}), bf16[16,32,256]{2,1,0:T(8,128)(2,1)S(1)}, u32[]{:S(2)}, u32[]{:S(2)}) async-start(bf16[16,32,256]{2,1,0:T(8,128)(2,1)} %get-tuple-element.39), calls=%async_computation.1 | async-start | bytes 524288 | tf_op jit(solution)/shard_map/all_to_all | solution.py:345
  50.1 8.9 %back_one.1 = (bf16[64,128,256]{2,1,0:T(8,128)(2,1)}, bf16[3,256,768]{2,1,0:T(8,128)(2,1)S(1)}, f32[8,128]{1,0:T(8,128)S(1)}) custom-call(bf16[64,128,256]{2,1,0:T(8,128)(2,1)} %bitcast.5, bf16[2,2,128,256]{3,2,1,0:T(8,128)(2,1)} %get-tuple-element.31.rim, bf16[2,68,2,256]{3,2,1,0:T(2,128)(2,1)} %get-tuple-element.32.pair_hbm, ...), custom_call_target="tpu_custom_call" | custom-call | flops 4831838208 | bytes 10109440 | tf_op jit(solution)/shard_map/back_one/pallas_call | solution.py:19
  59.0 0.0 all-to-all-done.1.got
  59.0 0.7 second.1
  59.7 7.4 %all-to-all-start.2 = ((bf16[16,16,256]{2,1,0:T(8,128)(2,1)}), bf16[16,16,256]{2,1,0:T(8,128)(2,1)S(1)}, u32[]{:S(2)}, u32[]{:S(2)}) async-start(bf16[16,16,256]{2,1,0:T(8,128)(2,1)} %second.1), calls=%async_computation.2 | async-start | bytes 262144 | tf_op jit(solution)/shard_map/all_to_all | solution.py:345
  67.1 8.9 %back_two.1 = bf16[64,128,256]{2,1,0:T(8,128)(2,1)} custom-call(bf16[64,128,256]{2,1,0:T(8,128)(2,1)} %bitcast.6, bf16[2,2,128,256]{3,2,1,0:T(8,128)(2,1)} %get-tuple-element.31.rim, bf16[2,68,2,256]{3,2,1,0:T(2,128)(2,1)} %get-tuple-element.32.pair_hbm, bf16[3,256,768]{2,1,0:T(8,128)(2,1)S(1)} %get-tuple-element.37.weights, ...), custom_call_target="tpu_custom_call", output_to_operand_aliasing={{}: (4, {})} | custom-call | flops 4831838208 | bytes 14163968 | tf_op jit(solution)/shard_map/back_two/pallas_call | solution.py:19
  76.0 0.0 all-to-all-done.2.got
  76.0 0.6 third.1
Async XLA Ops:
  1.9 4.2 %collective-permute-start = (bf16[65,2,256]{2,1,0:T(2,128)(2,1)S(1)}, bf16[65,2,256]{2,1,0:T(2,128)(2,1)S(1)}, u32[]{:S(2)}, u32[]{:S(2)}) collective-permute-start(bf16[65,2,256]{2,1,0:T(2,128)(2,1)S(1)} %get-tuple-element.23.mine), channel_id=1, source_target_pairs={{0,1},{1,0},{2,3},{3,2},{4,5},{5,4},{6,7},{7,6},{8,9},{9,8},{10,11... | collective-permute-start | bytes 199688 | tf_op jit(solution)/shard_map/ppermute | solution.py:341
  4.5 1.7 %collective-permute-start.1 = (bf16[65,2,256]{2,1,0:T(2,128)(2,1)S(1)}, bf16[65,2,256]{2,1,0:T(2,128)(2,1)S(1)}, u32[]{:S(2)}, u32[]{:S(2)}) collective-permute-start(bf16[65,2,256]{2,1,0:T(2,128)(2,1)S(1)} %get-tuple-element.26), channel_id=1, source_target_pairs={{1,2},{2,1},{5,6},{6,5},{9,10},{10,9},{13,14},{14,13},{17,18},{18,... | collective-permute-start | bytes 199688 | tf_op jit(solution)/shard_map/ppermute | solution.py:341
  7.6 22.7 %collective-permute-start.2 = (bf16[2,136,256]{2,1,0:T(8,128)(2,1)S(1)}, bf16[2,136,256]{2,1,0:T(8,128)(2,1)S(1)}, u32[]{:S(2)}, u32[]{:S(2)}) collective-permute-start(bf16[2,136,256]{2,1,0:T(8,128)(2,1)S(1)} %get-tuple-element.27), channel_id=1, source_target_pairs={{0,4},{4,0},{8,12},{12,8},{1,5},{5,1},{9,13},{13,9},{2,6},{6,2},{1... | collective-permute-start | bytes 417800 | tf_op jit(solution)/shard_map/ppermute | solution.py:341
  11.1 19.2 %collective-permute-start.3 = (bf16[2,136,256]{2,1,0:T(8,128)(2,1)S(1)}, bf16[2,136,256]{2,1,0:T(8,128)(2,1)S(1)}, u32[]{:S(2)}, u32[]{:S(2)}) collective-permute-start(bf16[2,136,256]{2,1,0:T(8,128)(2,1)S(1)} %get-tuple-element.28), channel_id=1, source_target_pairs={{4,8},{8,4},{5,9},{9,5},{6,10},{10,6},{7,11},{11,7},{20,24},{24,20... | collective-permute-start | bytes 417800 | tf_op jit(solution)/shard_map/ppermute | solution.py:341
  18.1 24.9 %all-to-all-start = ((bf16[128,2,256]{2,1,0:T(2,128)(2,1)}), bf16[128,2,256]{2,1,0:T(2,128)(2,1)S(1)}, u32[]{:S(2)}, u32[]{:S(2)}) async-start(bf16[128,2,256]{2,1,0:T(2,128)(2,1)} %get-tuple-element.34), calls=%async_computation | async-start | bytes 262144 | tf_op jit(solution)/shard_map/all_to_all | solution.py:345
  30.3 0.7 copy-start
  30.3 0.7 copy-start.1
  44.9 14.1 %all-to-all-start.1 = ((bf16[16,32,256]{2,1,0:T(8,128)(2,1)}), bf16[16,32,256]{2,1,0:T(8,128)(2,1)S(1)}, u32[]{:S(2)}, u32[]{:S(2)}) async-start(bf16[16,32,256]{2,1,0:T(8,128)(2,1)} %get-tuple-element.39), calls=%async_computation.1 | async-start | bytes 524288 | tf_op jit(solution)/shard_map/all_to_all | solution.py:345
  59.7 16.3 %all-to-all-start.2 = ((bf16[16,16,256]{2,1,0:T(8,128)(2,1)}), bf16[16,16,256]{2,1,0:T(8,128)(2,1)S(1)}, u32[]{:S(2)}, u32[]{:S(2)}) async-start(bf16[16,16,256]{2,1,0:T(8,128)(2,1)} %second.1), calls=%async_computation.2 | async-start | bytes 262144 | tf_op jit(solution)/shard_map/all_to_all | solution.py:345
